TPU v7x, 32 devices: a whole 2x2x4 slice. The times are simulated.
32 devices in a mesh: dp: 16 (over z, x, core), tensor: 2 (over y).
Axes of the slice: x: 2, y: 2, z: 4, core: 2. Of those that a mesh axis runs over, the one named last changes fastest.
Arguments:
- hidden_in: bfloat16 [4096, 768], P(('dp', 'tensor')), may hold values from -6 to 6
- out_grad: bfloat16 [4096, 768], P(('dp', 'tensor')), may hold values from -6 to 6
- segment_ids: int32 [16, 256], P('dp'), may hold values from 0 to 3, never falling along the last dimension, each value on 1 to 128 neighbouring positions
- norm_weight: float32 [768], replicated, may hold values from 0.5 to 1.5
- w_z: bfloat16 [768, 1536], P('dp', 'tensor'), may hold values from -0.21875 to 0.21875
- w_x: bfloat16 [768, 1536], P('dp', 'tensor'), may hold values from -0.21875 to 0.21875
- w_bc: bfloat16 [768, 256], P('dp'), may hold values from -0.21875 to 0.21875
- w_dt: bfloat16 [768, 24], P('dp', 'tensor'), may hold values from -0.21875 to 0.21875
- conv_x_w: float32 [4, 1536], P(None, 'tensor'), may hold values from -0.5 to 0.5
- conv_x_b: float32 [1536], P('tensor'), may hold values from -0.5 to 0.5
- conv_bc_w: float32 [4, 256], replicated, may hold values from -0.5 to 0.5
- conv_bc_b: float32 [256], replicated, may hold values from -0.5 to 0.5
- dt_bias: float32 [24], P('tensor'), may hold values from -6 to -2.5
- a_log: float32 [24], P('tensor'), may hold values from 0 to 2.77
- d_skip: float32 [24], P('tensor'), may hold values from 0.5 to 1.5
- gnorm_weight: float32 [1536], P('tensor'), may hold values from 0.5 to 1.5
- w_out: bfloat16 [1536, 768], P('tensor', 'dp'), may hold values from -0.15625 to 0.15625
Outputs:
- block_out: bfloat16 [4096, 768], P(('dp', 'tensor'))
- grad_hidden: float32 [4096, 768], P(('dp', 'tensor'))
- grad_norm_weight: float32 [768], replicated
- grad_w_z: float32 [768, 1536], P('dp', 'tensor')
- grad_w_x: float32 [768, 1536], P('dp', 'tensor')
- grad_w_bc: float32 [768, 256], P('dp')
- grad_w_dt: float32 [768, 24], P('dp', 'tensor')
- grad_conv_x_w: float32 [4, 1536], P(None, 'tensor')
- grad_conv_x_b: float32 [1536], P('tensor')
- grad_conv_bc_w: float32 [4, 256], replicated
- grad_conv_bc_b: float32 [256], replicated
- grad_dt_bias: float32 [24], P('tensor')
- grad_a_log: float32 [24], P('tensor')
- grad_d_skip: float32 [24], P('tensor')
- grad_gnorm_weight: float32 [1536], P('tensor')
- grad_w_out: float32 [1536, 768], P('tensor', 'dp')
Inputs may be any that keep to these rules, and one draw needn't show every extreme that they name: `segment_ids`: within a sequence the numbers start at 0, never fall and rise by one at each document start; each document has 1 to 128 tokens, one of them exactly 128.
All inputs are finite; a program needn't handle non-finite values.
Results may differ from a plain program's by a relative error of at most 0.017.
Values may be sent and summed in bfloat16 or wider, within the bound.
A program may use at most 128 MiB of HBM per device.

v0:
```python
from functools import partial

import jax
import jax.numpy as jnp
from jax import lax
from jax.experimental import pallas as pl
from jax.experimental.pallas import tpu as pltpu
from jax.sharding import PartitionSpec as P

GROUP = 256


epsilon = 1e-05


def shift_rows(values, offset):
    padding = jnp.zeros((offset, values.shape[1]), values.dtype)
    return jnp.concatenate([padding, values[:-offset]], axis=0)


def causal_conv(values, kernel, conv_bias, segments):
    kernel_taps = kernel.shape[0]
    summed = conv_bias[None, :] + kernel[kernel_taps - 1][None, :] * values
    for offset in range(1, kernel_taps):
        earlier = jnp.concatenate([jnp.full((offset,), -1, jnp.int32), segments[:-offset]])
        matches = (earlier == segments)[:, None]
        summed = summed + kernel[kernel_taps - 1 - offset][None, :] * jnp.where(
            matches, shift_rows(values, offset), 0.0
        )
    return jax.nn.silu(summed)


def group_scan(inputs, steps_dt, log_decay, in_state, out_state, segments, block_len):
    length, head_count, head_dim = inputs.shape
    blocks = length // block_len
    x_blocks = inputs.reshape(blocks, block_len, head_count, head_dim)
    dt_blocks = steps_dt.reshape(blocks, block_len, head_count)
    cum_decay = jnp.cumsum(log_decay.reshape(blocks, block_len, head_count), axis=1)
    b_blocks = in_state.reshape(blocks, block_len, -1)
    c_blocks = out_state.reshape(blocks, block_len, -1)
    seg_blocks = segments.reshape(blocks, block_len)
    positions = jnp.arange(block_len)
    causal = positions[:, None] >= positions[None, :]
    mask_intra = (causal[None] & (seg_blocks[:, :, None] == seg_blocks[:, None, :]))[:, None]
    scores = jnp.einsum("cqn,ckn->cqk", c_blocks, b_blocks, precision=lax.Precision.HIGHEST)
    cum_heads = cum_decay.transpose(0, 2, 1)
    differ = cum_heads[:, :, :, None] - cum_heads[:, :, None, :]
    decay_mat = jnp.where(mask_intra, jnp.exp(jnp.where(mask_intra, differ, 0.0)), 0.0)
    weights_mat = decay_mat * scores[:, None] * dt_blocks.transpose(0, 2, 1)[:, :, None, :]
    y_intra = jnp.einsum("chqk,ckhp->cqhp", weights_mat, x_blocks, precision=lax.Precision.HIGHEST)
    if blocks == 1:
        return y_intra.reshape(length, head_count, head_dim)
    last_seg = seg_blocks[:, -1]
    to_end = cum_decay[:, -1:, :] - cum_decay
    end_match = (seg_blocks == last_seg[:, None])[:, :, None]
    end_weight = jnp.where(end_match, jnp.exp(jnp.where(end_match, to_end, 0.0)), 0.0) * dt_blocks
    local_states = jnp.einsum(
        "ckh,ckhp,ckn->chpn", end_weight, x_blocks, b_blocks, precision=lax.Precision.HIGHEST
    )
    prev_last = jnp.concatenate([seg_blocks[:1, 0], last_seg[:-1]])
    carry_keep = jnp.where((last_seg == prev_last)[:, None], jnp.exp(cum_decay[:, -1, :]), 0.0)

    def advance(carried, packed):
        local_state, retain = packed
        return (retain[:, None, None] * carried + local_state, carried)

    zero_state = jnp.zeros(local_states.shape[1:], jnp.float32)
    _, entering = lax.scan(advance, zero_state, (local_states, carry_keep))
    start_match = (seg_blocks == prev_last[:, None])[:, :, None]
    start_weight = jnp.where(start_match, jnp.exp(cum_decay), 0.0)
    y_inter = (
        jnp.einsum("cqn,chpn->cqhp", c_blocks, entering, precision=lax.Precision.HIGHEST)
        * start_weight[..., None]
    )
    return (y_intra + y_inter).reshape(length, head_count, head_dim)


def mixer_core(
    z_proj,
    x_proj,
    bc_proj,
    dt_proj,
    conv_x_w,
    conv_x_b,
    conv_bc_w,
    conv_bc_b,
    dt_bias,
    a_log,
    d_skip,
    segments,
    block_len,
):
    head_count = dt_proj.shape[1]
    head_dim = x_proj.shape[1] // head_count
    state_dim = bc_proj.shape[1] // 2
    x_conv = causal_conv(x_proj, conv_x_w, conv_x_b, segments)
    bc_conv = causal_conv(bc_proj, conv_bc_w, conv_bc_b, segments)
    steps_dt = jax.nn.softplus(dt_proj + dt_bias[None, :])
    log_decay = -jnp.exp(a_log)[None, :] * steps_dt
    x_heads = x_conv.reshape(-1, head_count, head_dim)
    scanned = group_scan(
        x_heads,
        steps_dt,
        log_decay,
        bc_conv[:, :state_dim],
        bc_conv[:, state_dim:],
        segments,
        block_len,
    )
    y_heads = scanned + d_skip[None, :, None] * x_heads
    return y_heads.reshape(x_proj.shape) * jax.nn.silu(z_proj)


F32 = jnp.float32
BF16 = jnp.bfloat16
MESH = pl.DeviceIdType.MESH


def ring_order(count):
    near = [1, count - 1] if count > 2 else [1]
    return [k for k in near if 0 < k < count] + list(range(2, count - 1))


def place(n):
    me = lax.axis_index("dp")
    return me, me // 4, (me // 2) % 2, me % 2


def greet(peers):
    barrier = pltpu.get_barrier_semaphore()
    for peer in peers:
        pl.semaphore_signal(barrier, inc=1, device_id=peer, device_id_type=MESH)
    pl.semaphore_wait(barrier, len(peers))


def remote(src, dst, send_sem, recv_sem, peer):
    return pltpu.make_async_remote_copy(
        src_ref=src,
        dst_ref=dst,
        send_sem=send_sem,
        recv_sem=recv_sem,
        device_id=peer,
        device_id_type=MESH,
    )


def peers_of(n, nt):
    me, z, x, c = place(n)
    t = lax.axis_index("tensor")
    zs = n // 4
    z_peer = {k: (((z + k) % zs) * 4 + x * 2 + c, t) for k in range(1, zs)}
    x_peer = (z * 4 + (1 - x) * 2 + c, t)
    c_peer = (z * 4 + x * 2 + (1 - c), t)
    t_peer = {k: (me, (t + k) % nt) for k in range(1, nt)}
    return z_peer, x_peer, c_peer, t_peer


def gather_body(n, nt, w_ref, h_ref, o_ref, w_all, h_all, o_all,
                zs_sem, zr_sem, xs_sem, xr_sem, cs_sem, cr_sem, ts_sem, tr_sem):
    me, z, x, c = place(n)
    t = lax.axis_index("tensor")
    zn = n // 4
    z_peer, x_peer, c_peer, t_peer = peers_of(n, nt)
    greet(list(z_peer.values()) + [x_peer, c_peer] + list(t_peer.values()))
    above, below = z_peer[1], z_peer[zn - 1]
    has_above, has_below = z < zn - 1, z > 0
    started = []

    def go(src, dst, send_sem, recv_sem, peer):
        copy = remote(src, dst, send_sem, recv_sem, peer)
        copy.start()
        started.append(copy)

    def z_go(src, dst, level, up):
        copy = remote(src, dst, zs_sem.at[level + (0 if up else zn)], zr_sem.at[level],
                      above if up else below)
        copy.start()

    @pl.when(has_above)
    def _():
        z_go(w_ref, w_all.at[me], z, True)

    @pl.when(has_below)
    def _():
        z_go(w_ref, w_all.at[me], z, False)

    remote(w_ref, w_all.at[me], xs_sem.at[z], xr_sem.at[z], x_peer).start()
    remote(w_ref, w_all.at[me], cs_sem.at[z], cr_sem.at[z], c_peer).start()
    for k in range(1, nt):
        go(h_ref, h_all.at[t], ts_sem.at[k], tr_sem.at[k], t_peer[k])
        go(o_ref, o_all.at[t], ts_sem.at[nt + k], tr_sem.at[nt + k], t_peer[k])
    w_all[pl.ds(me, 1)] = w_ref[...][None]
    h_all[pl.ds(t, 1)] = h_ref[...][None]
    o_all[pl.ds(t, 1)] = o_ref[...][None]

    def take(level, up):
        got = w_all.at[level * 4 + x * 2 + c]
        remote(got, got, zs_sem.at[level], zr_sem.at[level], above).wait_recv()

        @pl.when(has_above if up else has_below)
        def _():
            z_go(got, got, level, up)

        remote(got, got, xs_sem.at[level], xr_sem.at[level], x_peer).start()
        remote(got, got, cs_sem.at[level], cr_sem.at[level], c_peer).start()

    def cross(level):
        got = w_all.at[level * 4 + (1 - x) * 2 + c]
        remote(got, got, xs_sem.at[level], xr_sem.at[level], x_peer).wait_recv()
        remote(got, got, cs_sem.at[zn + level], cr_sem.at[zn + level], c_peer).start()

    def by_distance(visit):
        for s in range(1, zn):
            @pl.when(z - s >= 0)
            def _(s=s):
                visit(z - s, True)

            @pl.when(z + s < zn)
            def _(s=s):
                visit(z + s, False)

    by_distance(take)
    cross(z)
    by_distance(lambda level, up: cross(level))
    for half in range(2):
        side = x if half == 0 else 1 - x
        for level in range(zn):
            got = w_all.at[level * 4 + side * 2 + (1 - c)]
            j = half * zn + level
            remote(got, got, cs_sem.at[j], cr_sem.at[j], c_peer).wait_recv()
    for k in range(1, nt):
        got_h = h_all.at[(t + nt - k) % nt]
        got_o = o_all.at[(t + nt - k) % nt]
        remote(got_h, got_h, ts_sem.at[k], tr_sem.at[k], t_peer[k]).wait_recv()
        remote(got_o, got_o, ts_sem.at[nt + k], tr_sem.at[nt + k], t_peer[k]).wait_recv()
    for copy in started:
        copy.wait_send()
    for level in range(zn):
        sent = w_all.at[level * 4 + x * 2 + c]
        crossed = w_all.at[level * 4 + (1 - x) * 2 + c]
        remote(sent, sent, xs_sem.at[level], xr_sem.at[level], x_peer).wait_send()
        remote(sent, sent, cs_sem.at[level], cr_sem.at[level], c_peer).wait_send()
        remote(crossed, crossed, cs_sem.at[zn + level], cr_sem.at[zn + level], c_peer).wait_send()

        @pl.when((level <= z) & has_above)
        def _(level=level, sent=sent):
            remote(sent, sent, zs_sem.at[level], zr_sem.at[level], above).wait_send()

        @pl.when((level >= z) & has_below)
        def _(level=level, sent=sent):
            remote(sent, sent, zs_sem.at[zn + level], zr_sem.at[level], below).wait_send()


VM = pl.BlockSpec(memory_space=pltpu.VMEM)
DMA = pltpu.SemaphoreType.DMA


def gather_all(w_pack, hidden, cot):
    n, nt = lax.axis_size("dp"), lax.axis_size("tensor")
    zn = n // 4
    return pl.pallas_call(
        partial(gather_body, n, nt),
        out_shape=(
            jax.ShapeDtypeStruct((n,) + w_pack.shape, BF16),
            jax.ShapeDtypeStruct((nt,) + hidden.shape, BF16),
            jax.ShapeDtypeStruct((nt,) + cot.shape, BF16),
        ),
        in_specs=[VM] * 3,
        out_specs=(VM,) * 3,
        scratch_shapes=[
            DMA((2 * zn,)), DMA((zn,)), DMA((zn,)), DMA((zn,)),
            DMA((2 * zn,)), DMA((2 * zn,)), DMA((2 * nt,)), DMA((2 * nt,)),
        ],
        compiler_params=pltpu.CompilerParams(collective_id=0, has_side_effects=True),
        name="gather_all",
    )(w_pack, hidden, cot)


def pair_body(nt, p_ref, out_ref, got_ref, s_sem, r_sem):
    me = lax.axis_index("dp")
    t = lax.axis_index("tensor")
    peers = {k: (me, (t + k) % nt) for k in range(1, nt)}
    greet(list(peers.values()))
    copies = []
    for k in range(1, nt):
        copy = remote(p_ref, got_ref.at[t], s_sem.at[k], r_sem.at[k], peers[k])
        copy.start()
        copies.append(copy)
    got_ref[pl.ds(t, 1)] = p_ref[...][None]
    for k in range(1, nt):
        got = got_ref.at[(t + nt - k) % nt]
        remote(got, got, s_sem.at[k], r_sem.at[k], peers[k]).wait_recv()
    total = got_ref[0]
    for i in range(1, nt):
        total = total + got_ref[i]
    out_ref[...] = total
    for copy in copies:
        copy.wait_send()


def tensor_sum(values):
    nt = lax.axis_size("tensor")
    return pl.pallas_call(
        partial(pair_body, nt),
        out_shape=jax.ShapeDtypeStruct(values.shape, F32),
        in_specs=[VM],
        out_specs=VM,
        scratch_shapes=[pltpu.VMEM((nt,) + values.shape, F32), DMA((nt,)), DMA((nt,))],
        compiler_params=pltpu.CompilerParams(collective_id=1, has_side_effects=True),
        name="tensor_sum",
    )(values)


def reduce_body(n, nt, bc_width, g_ref, dn_ref, op_ref, sl_ref, ss_ref,
                g_out, dn_out, op_out, sl_out, ss_out,
                c_got, x_put, x_got, z_put, z_got, dn_got, op_got, bc_put, bc_got,
                sl_c, sl_xput, sl_x, sl_z, ss_t, ss_cput, ss_c, ss_xput, ss_x, ss_z,
                cs, cr, xs, xr, zs, zr, ts, tr):
    me, z, x, c = place(n)
    t = lax.axis_index("tensor")
    zn = n // 4
    z_peer, x_peer, c_peer, t_peer = peers_of(n, nt)
    order = ring_order(zn)
    order = order[2:] + order[:2]
    greet(list(z_peer.values()) + [x_peer, c_peer] + list(t_peer.values()))
    started = []

    def go(src, dst, send_sem, recv_sem, peer):
        copy = remote(src, dst, send_sem, recv_sem, peer)
        copy.start()
        started.append(copy)

    def arrived(dst, send_sem, recv_sem, peer):
        remote(dst, dst, send_sem, recv_sem, peer).wait_recv()

    def mine(k, side, core):
        return ((z + k) % zn) * 4 + side * 2 + core

    go(sl_ref, sl_c, cs.at[2 * zn], cr.at[2 * zn], c_peer)
    for k in range(1, nt):
        go(ss_ref, ss_t.at[t], ts.at[k], tr.at[k], t_peer[k])
    zorder = order + [0]
    for half in range(2):
        side = 1 - x if half == 0 else x
        for k in zorder:
            j = half * zn + k
            go(g_ref.at[mine(k, side, 1 - c)], c_got.at[j], cs.at[j], cr.at[j], c_peer)
    for k in range(1, nt):
        peer_t = (t + k) % nt
        go(dn_ref.at[peer_t], dn_got.at[t], ts.at[nt + k], tr.at[nt + k], t_peer[k])
        go(op_ref.at[peer_t], op_got.at[t], ts.at[2 * nt + k], tr.at[2 * nt + k], t_peer[k])
    ss_t[pl.ds(t, 1)] = ss_ref[...][None]

    def x_send(k):
        arrived(c_got.at[k], cs.at[k], cr.at[k], c_peer)
        part = g_ref[mine(k, 1 - x, c)].astype(F32) + c_got[k].astype(F32)
        x_put[k] = part.astype(BF16)
        go(x_put.at[k], x_got.at[k], xs.at[k], xr.at[k], x_peer)

    for k in zorder[:1]:
        x_send(k)
    arrived(sl_c, cs.at[2 * zn], cr.at[2 * zn], c_peer)
    sl_xput[...] = sl_ref[...] + sl_c[...]
    go(sl_xput, sl_x, xs.at[zn], xr.at[zn], x_peer)
    for k in range(1, nt):
        got = ss_t.at[(t + nt - k) % nt]
        arrived(got, ts.at[k], tr.at[k], t_peer[k])
    total = ss_t[0]
    for i in range(1, nt):
        total = total + ss_t[i]
    ss_cput[...] = total
    go(ss_cput, ss_c, cs.at[2 * zn + 1], cr.at[2 * zn + 1], c_peer)
    for k in zorder[1:2]:
        x_send(k)
    arrived(ss_c, cs.at[2 * zn + 1], cr.at[2 * zn + 1], c_peer)
    ss_xput[...] = ss_cput[...] + ss_c[...]
    go(ss_xput, ss_x, xs.at[zn + 1], xr.at[zn + 1], x_peer)
    for k in zorder[2:]:
        x_send(k)

    def z_send(k):
        j = zn + k
        arrived(c_got.at[j], cs.at[j], cr.at[j], c_peer)
        part = g_ref[mine(k, x, c)].astype(F32) + c_got[j].astype(F32)
        arrived(x_got.at[k], xs.at[k], xr.at[k], x_peer)
        part = part + x_got[k].astype(F32)
        if k == 0:
            g_out[...] = part
        else:
            z_put[k] = part.astype(BF16)
            go(z_put.at[k], z_got.at[k], zs.at[k], zr.at[k], z_peer[k])

    for k in zorder[:1]:
        z_send(k)
    arrived(sl_x, xs.at[zn], xr.at[zn], x_peer)
    sl_z[pl.ds(z, 1)] = (sl_xput[...] + sl_x[...])[None]
    for k in order:
        go(sl_z.at[z], sl_z.at[z], zs.at[zn + k], zr.at[zn + k], z_peer[k])
    arrived(ss_x, xs.at[zn + 1], xr.at[zn + 1], x_peer)
    ss_z[pl.ds(z, 1)] = (ss_xput[...] + ss_x[...])[None]
    for k in order:
        go(ss_z.at[z], ss_z.at[z], zs.at[2 * zn + k], zr.at[2 * zn + k], z_peer[k])
    for k in zorder[1:]:
        z_send(k)

    dn_total = dn_ref[t].astype(F32)
    op_total = op_ref[t].astype(F32)
    for k in range(1, nt):
        slot = (t + nt - k) % nt
        arrived(dn_got.at[slot], ts.at[nt + k], tr.at[nt + k], t_peer[k])
        arrived(op_got.at[slot], ts.at[2 * nt + k], tr.at[2 * nt + k], t_peer[k])
        dn_total = dn_total + dn_got[slot].astype(F32)
        op_total = op_total + op_got[slot].astype(F32)
    dn_out[...] = dn_total
    op_out[...] = op_total

    for k in order:
        slot = sl_z.at[(z + zn - k) % zn]
        arrived(slot, zs.at[zn + k], zr.at[zn + k], z_peer[k])
        slot = ss_z.at[(z + zn - k) % zn]
        arrived(slot, zs.at[2 * zn + k], zr.at[2 * zn + k], z_peer[k])
    sl_total, ss_total = sl_z[0], ss_z[0]
    for i in range(1, zn):
        sl_total = sl_total + sl_z[i]
        ss_total = ss_total + ss_z[i]
    sl_out[...] = sl_total
    ss_out[...] = ss_total

    for k in order:
        arrived(z_got.at[k], zs.at[k], zr.at[k], z_peer[k])
        g_out[...] += z_got[k].astype(F32)
    bc_put[...] = g_out[:, :bc_width].astype(BF16)
    for k in range(1, nt):
        go(bc_put, bc_got.at[t], ts.at[3 * nt + k], tr.at[3 * nt + k], t_peer[k])
    bc_got[pl.ds(t, 1)] = bc_put[...][None]
    for k in range(1, nt):
        got = bc_got.at[(t + nt - k) % nt]
        arrived(got, ts.at[3 * nt + k], tr.at[3 * nt + k], t_peer[k])
    total = bc_got[0].astype(F32)
    for i in range(1, nt):
        total = total + bc_got[i].astype(F32)
    g_out[:, :bc_width] = total
    for copy in started:
        copy.wait_send()


def reduce_all(grads, dn_part, out_part, small_loc, small_sh, bc_width):
    n, nt = lax.axis_size("dp"), lax.axis_size("tensor")
    zn = n // 4
    shard = grads.shape[1:]
    rows = dn_part.shape[1:]
    sl, ss = small_loc.shape, small_sh.shape
    V = pltpu.VMEM
    return pl.pallas_call(
        partial(reduce_body, n, nt, bc_width),
        out_shape=(
            jax.ShapeDtypeStruct(shard, F32),
            jax.ShapeDtypeStruct(rows, F32),
            jax.ShapeDtypeStruct(rows, F32),
            jax.ShapeDtypeStruct(sl, F32),
            jax.ShapeDtypeStruct(ss, F32),
        ),
        in_specs=[VM] * 5,
        out_specs=(VM,) * 5,
        scratch_shapes=[
            V((2 * zn,) + shard, BF16), V((zn,) + shard, BF16), V((zn,) + shard, BF16),
            V((zn,) + shard, BF16), V((zn,) + shard, BF16),
            V((nt,) + rows, BF16), V((nt,) + rows, BF16),
            V((shard[0], bc_width), BF16), V((nt, shard[0], bc_width), BF16),
            V(sl, F32), V(sl, F32), V(sl, F32), V((zn,) + sl, F32),
            V((nt,) + ss, F32), V(ss, F32), V(ss, F32), V(ss, F32), V(ss, F32), V((zn,) + ss, F32),
            DMA((2 * zn + 2,)), DMA((2 * zn + 2,)), DMA((zn + 2,)), DMA((zn + 2,)),
            DMA((3 * zn,)), DMA((3 * zn,)), DMA((4 * nt,)), DMA((4 * nt,)),
        ],
        compiler_params=pltpu.CompilerParams(collective_id=2, has_side_effects=True),
        name="reduce_all",
    )(grads, dn_part, out_part, small_loc, small_sh)


def pad_columns(values, width):
    return jnp.pad(values, ((0, 0), (0, width - values.shape[1])))


HIGH = lax.Precision.HIGHEST


def mm(a, b, dims=((1,), (0,)), precision=None):
    return lax.dot_general(a, b, (dims, ((), ())), precision=precision, preferred_element_type=F32)


def row_shift(values, offset):
    return pltpu.roll(values, offset % values.shape[0], axis=0)


def sigmoid(values):
    return 1.0 / (1.0 + jnp.exp(-values))


def conv_masks(seg_col, taps):
    length = seg_col.shape[0]
    seg_wide = jnp.broadcast_to(seg_col, (length, 128))
    position = lax.broadcasted_iota(jnp.int32, (length, 128), 0)
    masks = [None]
    for o in range(1, taps):
        same = (row_shift(seg_wide, o) == seg_wide) & (position >= o)
        masks.append(jnp.where(same, 1.0, 0.0)[:, :1])
    return masks


def conv_pre(values, kernel, bias, masks):
    taps = kernel.shape[0]
    total = bias + kernel[taps - 1 : taps] * values
    for o in range(1, taps):
        total = total + kernel[taps - 1 - o : taps - o] * (masks[o] * row_shift(values, o))
    return total


def conv_back(d_pre, values, kernel, masks):
    taps = kernel.shape[0]
    d_values = kernel[taps - 1 : taps] * d_pre
    rows = [jnp.sum(d_pre * values, axis=0, keepdims=True)]
    for o in range(1, taps):
        masked = masks[o] * d_pre
        rows.append(jnp.sum(masked * row_shift(values, o), axis=0, keepdims=True))
        d_values = d_values + kernel[taps - 1 - o : taps - o] * row_shift(masked, -o)
    return d_values, rows[::-1], jnp.sum(d_pre, axis=0, keepdims=True)


def head_map(lanes, channels, head_dim):
    head = lax.broadcasted_iota(jnp.int32, (lanes, channels), 0)
    channel = lax.broadcasted_iota(jnp.int32, (lanes, channels), 1)
    return jnp.where(channel // head_dim == head, 1.0, 0.0)


def scan_setup(p_ref, seg_col, seg_row, cxw, cxb, cbw, cbb, dtb, alog, z0, bc_width, inner):
    masks = conv_masks(seg_col, cxw.shape[0])
    length = seg_col.shape[0]
    x_raw = p_ref[:, z0 + inner : z0 + 2 * inner]
    bc_raw = p_ref[:, :bc_width]
    x_pre = conv_pre(x_raw, cxw, cxb, masks)
    bc_pre = conv_pre(bc_raw, cbw, cbb, masks)
    u = p_ref[:, bc_width:z0] + dtb
    step = jnp.maximum(u, 0.0) + jnp.log1p(jnp.exp(-jnp.abs(u)))
    rate = -jnp.exp(alog)
    log_decay = rate * step
    row = lax.broadcasted_iota(jnp.int32, (length, length), 0)
    col = lax.broadcasted_iota(jnp.int32, (length, length), 1)
    lower = jnp.where(row >= col, 1.0, 0.0)
    cum = mm(lower, log_decay, precision=HIGH)
    allowed = (row >= col) & (seg_col == seg_row)
    return masks, x_raw, bc_raw, x_pre, bc_pre, u, step, rate, cum, allowed, row, col


def core_fwd_body(heads, inner, bc_width, z0, w_ref, hid_ref, cot_ref, segc_ref, segr, cxw, cbw, vec,
                  p_out, y_out, back_out, norm_out, sum_out):
    nw, cxb, gnw = vec[0:1, : hid_ref.shape[1]], vec[1:2, :inner], vec[2:3, :inner]
    cbb, dtb = vec[3:4, :bc_width], vec[4:5, : z0 - bc_width]
    alog, dskip = vec[5:6, : z0 - bc_width], vec[6:7, : z0 - bc_width]
    segc = segc_ref[:, :1]
    head_dim = inner // heads
    hid = hid_ref[...].astype(F32)
    rms = lax.rsqrt(jnp.mean(hid * hid, axis=1, keepdims=True) + epsilon)
    norm_out[...] = (hid * rms * nw).astype(BF16)
    p_out[...] = mm(norm_out[...], w_ref[:, : z0 + 2 * inner])
    back_out[...] = mm(cot_ref[...], w_ref[:, z0 + 2 * inner :])
    (_, _, _, x_pre, bc_pre, _, step, _, cum, allowed, _, _) = scan_setup(
        p_out, segc, segr[...].astype(F32), cxw[...], cxb, cbw[...], cbb, dtb, alog,
        z0, bc_width, inner)
    spread = head_map(step.shape[1], inner, head_dim)
    x_conv = x_pre * sigmoid(x_pre)
    bc_conv = (bc_pre * sigmoid(bc_pre)).astype(BF16)
    state = bc_width // 2
    scores = mm(bc_conv[:, state:], bc_conv[:, :state], ((1,), (1,)))
    scores = jnp.where(allowed, scores, 0.0)
    x_step = (x_conv * mm(step, spread, precision=HIGH)).astype(BF16)
    skip = mm(jnp.broadcast_to(dskip, (8, step.shape[1])), spread, precision=HIGH)[:1]
    cum_t = cum.T
    per = 128 // head_dim
    for g in range(heads // per):
        cols = slice(g * 128, (g + 1) * 128)
        lane = lax.broadcasted_iota(jnp.int32, (x_step.shape[0], 128), 1)
        part = None
        for i in range(per):
            h = g * per + i
            decay = jnp.exp(jnp.where(allowed, cum[:, h : h + 1] - cum_t[h : h + 1, :], 0.0))
            one = mm((decay * scores).astype(BF16), x_step[:, cols])
            part = one if part is None else jnp.where(lane < i * head_dim, part, one)
        y_out[:, cols] = part + skip[:, cols] * x_conv[:, cols]
    z = p_out[:, z0 : z0 + inner]
    gated = y_out[...] * (z * sigmoid(z))
    sq = jnp.sum(gated * gated, axis=1, keepdims=True)
    dot = jnp.sum(back_out[...] * gated * gnw, axis=1, keepdims=True)
    lane = lax.broadcasted_iota(jnp.int32, (gated.shape[0], 128), 1)
    both = jnp.where(lane == 0, sq, jnp.where(lane == 1, dot, 0.0))
    sum_out[...] = both.T[:8]


def core_bwd_body(heads, inner, inner_all, bc_width, z0, w_ref, hid_ref, cot_ref, segc_ref, segr, cxw, cbw, vec, p_ref, y_ref, back_ref, norm_ref, sum_ref,
                  grad_out, dn_out, op_out, loc_out, sh_out, gate_out, dy_s, dx_s, dproj_s):
    nw, cxb, gnw = vec[0:1, : hid_ref.shape[1]], vec[1:2, :inner], vec[2:3, :inner]
    cbb, dtb = vec[3:4, :bc_width], vec[4:5, : z0 - bc_width]
    alog, dskip = vec[5:6, : z0 - bc_width], vec[6:7, : z0 - bc_width]
    segc = segc_ref[:, :1]
    head_dim = inner // heads
    state = bc_width // 2
    length = segc.shape[0]
    taps = cxw.shape[0]
    sums = jnp.concatenate([sum_ref[...], jnp.zeros((120, length), F32)], axis=0).T
    inv = lax.rsqrt(sums[:, :1] / inner_all + epsilon)
    gate_out[...] = jnp.broadcast_to(inv, (length, 128))
    coef = sums[:, 1:2] * (inv * inv * inv) / inner_all
    z = p_ref[:, z0 : z0 + inner]
    z_sig = sigmoid(z)
    z_silu = z * z_sig
    y = y_ref[...]
    gated = y * z_silu
    grad_q = inv * back_ref[...]
    loc_out[...] = jnp.zeros(loc_out.shape, F32)
    sh_out[...] = jnp.zeros(sh_out.shape, F32)
    loc_out[taps + 1 : taps + 2, :] = jnp.sum(grad_q * gated, axis=0, keepdims=True)
    scaled = (gated * gnw).astype(BF16)
    op_out[...] = mm(scaled, w_ref[:, z0 + 2 * inner :], ((1,), (1,))).astype(BF16)
    scaled_out = (inv * scaled.astype(F32)).astype(BF16)
    grad_out[:, z0 + 2 * inner :] = mm(cot_ref[...], scaled_out, ((0,), (0,))).astype(BF16)
    d_gated = grad_q * gnw - coef * gated
    dy_s[...] = d_gated * z_silu
    dproj_s[:, z0 : z0 + inner] = (d_gated * y * (z_sig * (1.0 + z * (1.0 - z_sig)))).astype(BF16)

    (masks, x_raw, bc_raw, x_pre, bc_pre, u, step, rate, cum, allowed, row, col) = scan_setup(
        p_ref, segc, segr[...].astype(F32), cxw[...], cxb, cbw[...], cbb, dtb, alog,
        z0, bc_width, inner)
    lanes = step.shape[1]
    spread = head_map(lanes, inner, head_dim)
    x_sig = sigmoid(x_pre)
    x_conv = x_pre * x_sig
    bc_sig = sigmoid(bc_pre)
    bc_conv = (bc_pre * bc_sig).astype(BF16)
    b_state, c_state = bc_conv[:, :state], bc_conv[:, state:]
    scores = jnp.where(allowed, mm(c_state, b_state, ((1,), (1,))), 0.0)
    step_wide = mm(step, spread, precision=HIGH)
    x_step = (x_conv * step_wide).astype(BF16)
    skip = mm(jnp.broadcast_to(dskip, (8, lanes)), spread, precision=HIGH)[:1]
    cum_t = cum.T
    per = 128 // head_dim
    lane = lax.broadcasted_iota(jnp.int32, (length, 128), 1)
    d_scores = jnp.zeros((length, length), F32)
    row_sums = jnp.zeros((length, 128), F32)
    col_sums = []
    for g in range(heads // per):
        cols = slice(g * 128, (g + 1) * 128)
        dy = dy_s[:, cols]
        dy_b = dy.astype(BF16)
        part = None
        for i in range(per):
            h = g * per + i
            inside = (lane >= i * head_dim) & (lane < (i + 1) * head_dim)
            decay = jnp.where(
                allowed, jnp.exp(jnp.where(allowed, cum[:, h : h + 1] - cum_t[h : h + 1, :], 0.0)), 0.0)
            weight = decay * scores
            d_weight = mm(jnp.where(inside, dy, 0.0).astype(BF16), x_step[:, cols], ((1,), (1,)))
            d_scores = d_scores + d_weight * decay
            flow = d_weight * weight
            row_sums = jnp.where(lane == h, jnp.sum(flow, axis=1, keepdims=True), row_sums)
            col_sums.append(jnp.sum(flow, axis=0, keepdims=True))
            one = mm(weight.astype(BF16), dy_b, ((0,), (0,)))
            part = one if part is None else jnp.where(lane < i * head_dim, part, one)
        dx_s[:, cols] = part
    col_rows = jnp.concatenate(col_sums + [jnp.zeros((128 - heads, length), F32)], axis=0)
    d_cum = row_sums - col_rows.T
    d_log = mm(jnp.where(row <= col, 1.0, 0.0), d_cum, precision=HIGH)
    d_xs = dx_s[...]
    dy = dy_s[...]
    d_step = mm((d_xs * x_conv).astype(BF16), spread.astype(BF16), ((1,), (1,)))
    d_step = d_step + rate * d_log
    d_u = d_step * sigmoid(u)
    skip_row = jnp.sum(dy * x_conv, axis=0, keepdims=True)
    d_skip = mm(jnp.broadcast_to(skip_row, (8, inner)), spread, ((1,), (1,)), precision=HIGH)[:1]
    loc_out[taps + 2 : taps + 3, :lanes] = jnp.sum(d_u, axis=0, keepdims=True)
    loc_out[taps + 3 : taps + 4, :lanes] = rate * jnp.sum(d_log * step, axis=0, keepdims=True)
    loc_out[taps + 4 : taps + 5, :lanes] = d_skip
    head_lane = lax.broadcasted_iota(jnp.int32, (length, lanes), 1)
    dproj_s[:, bc_width:z0] = jnp.where(head_lane < heads, d_u, 0.0).astype(BF16)

    d_xpre = (d_xs * step_wide + skip * dy) * (x_sig * (1.0 + x_pre * (1.0 - x_sig)))
    d_x, rows, bias_row = conv_back(d_xpre, x_raw, cxw[...], masks)
    dproj_s[:, z0 + inner : z0 + 2 * inner] = d_x.astype(BF16)
    for k in range(taps):
        loc_out[k : k + 1, :] = rows[k]
    loc_out[taps : taps + 1, :] = bias_row

    d_scores = d_scores.astype(BF16)
    d_b = mm(d_scores, c_state, ((0,), (0,)))
    d_c = mm(d_scores, b_state)
    d_bcpre = jnp.concatenate([d_b, d_c], axis=1) * (bc_sig * (1.0 + bc_pre * (1.0 - bc_sig)))
    d_bc, rows, bias_row = conv_back(d_bcpre, bc_raw, cbw[...], masks)
    dproj_s[:, :bc_width] = d_bc.astype(BF16)
    for k in range(taps):
        sh_out[k : k + 1, :bc_width] = rows[k]
    sh_out[taps : taps + 1, :bc_width] = bias_row

    d_proj = dproj_s[...]
    grad_out[:, : z0 + 2 * inner] = mm(norm_ref[...], d_proj, ((0,), (0,))).astype(BF16)
    d_normed = mm(d_proj, w_ref[:, : z0 + 2 * inner], ((1,), (1,)))
    dn_out[...] = d_normed.astype(BF16)
    hid = hid_ref[...].astype(F32)
    rms = lax.rsqrt(jnp.mean(hid * hid, axis=1, keepdims=True) + epsilon)
    sh_out[taps + 1 : taps + 2, :] = jnp.sum(d_normed * (hid * rms), axis=0, keepdims=True)


def prepare_body(heads, bc_width, z0, inner, wz, wx, wbc, wdt, wout, seg, nw, cxb, gnw, cbb, dtb, alog,
                 dskip, pack, vec, segc):
    rows = wz.shape[0]
    pack[:, :bc_width] = wbc[...]
    pack[:, bc_width:z0] = jnp.zeros((rows, z0 - bc_width), BF16)
    pack[:, bc_width : bc_width + heads] = wdt[...]
    pack[:, z0 : z0 + inner] = wz[...]
    pack[:, z0 + inner : z0 + 2 * inner] = wx[...]
    pack[:, z0 + 2 * inner :] = wout[...]
    vec[...] = jnp.zeros(vec.shape, F32)
    for i, ref in enumerate((nw, cxb, gnw, cbb, dtb, alog, dskip)):
        vec[i : i + 1, : ref.shape[0]] = ref[...][None, :]
    segc[...] = jnp.broadcast_to(seg[...].astype(F32), (128, seg.shape[1])).T


def prepare(w_z, w_x, w_bc, w_dt, w_out, segments, vectors, z0):
    rows, inner = w_z.shape
    width = max(inner, max(v.shape[0] for v in vectors))
    length = segments.shape[1]
    return pl.pallas_call(
        partial(prepare_body, w_dt.shape[1], w_bc.shape[1], z0, inner),
        out_shape=(
            jax.ShapeDtypeStruct((rows, z0 + 3 * inner), BF16),
            jax.ShapeDtypeStruct((8, width), F32),
            jax.ShapeDtypeStruct((length, 128), F32),
        ),
        in_specs=[VM] * 13,
        out_specs=(VM,) * 3,
        name="prepare",
    )(w_z, w_x, w_bc, w_dt, w_out.T, segments, *vectors)


def fused_core(w_full, hid, cot, segments, seg_col, conv_x_w, conv_bc_w, vec, heads, inner,
               inner_all, bc_width, z0):
    length, width = hid.shape
    taps = conv_x_w.shape[0]

    def sds(shape, dtype=F32):
        return jax.ShapeDtypeStruct(shape, dtype)

    small = (conv_x_w, conv_bc_w, vec)
    cols = z0 + 2 * inner
    saved = pl.pallas_call(
        partial(core_fwd_body, heads, inner, bc_width, z0),
        out_shape=(sds((length, cols)), sds((length, inner)), sds((length, inner)),
                   sds((length, width), BF16), sds((8, length))),
        in_specs=[VM] * 8,
        out_specs=(VM,) * 5,
        name="core_fwd",
    )(w_full, hid, cot, seg_col, segments, *small)
    sums = tensor_sum(saved[4])
    return pl.pallas_call(
        partial(core_bwd_body, heads, inner, inner_all, bc_width, z0),
        out_shape=(sds(w_full.shape, BF16), sds((length, width), BF16), sds((length, width), BF16),
                   sds((taps + 5, inner)), sds((taps + 2, width)), sds((length, 128))),
        in_specs=[VM] * 13,
        out_specs=(VM,) * 6,
        scratch_shapes=[pltpu.VMEM((length, inner), F32), pltpu.VMEM((length, inner), F32),
                        pltpu.VMEM((length, cols), BF16)],
        name="core_bwd",
    )(w_full, hid, cot, seg_col, segments, *small, *saved[:4], sums)


def finish_body(heads, bc_width, z0, inner, taps, g, dn, op, sl, ss, hidden, cot, gate, vec,
                block, ghid, gnorm_in, gz, gx, gbc, gdt, gcxw, gcxb, gcbw, gcbb, gdtb, galog, gskip,
                ggn, gout):
    rows, width = hidden.shape
    start = pl.multiple_of(lax.axis_index("tensor") * rows, rows)
    hid = hidden[...].astype(F32)
    rms = lax.rsqrt(jnp.mean(hid * hid, axis=1, keepdims=True) + epsilon)
    block[...] = (hid + gate[pl.ds(start, rows), :][:, :1] * op[...]).astype(BF16)
    d_scaled = dn[...] * vec[0:1, :width]
    cube = rms * rms * rms
    ghid[...] = (
        cot[...].astype(F32)
        + rms * d_scaled
        - cube * hid * jnp.mean(d_scaled * hid, axis=1, keepdims=True)
    )
    gbc[...] = g[:, :bc_width]
    gdt[...] = g[:, bc_width : bc_width + heads]
    gz[...] = g[:, z0 : z0 + inner]
    gx[...] = g[:, z0 + inner : z0 + 2 * inner]
    gout[...] = g[:, z0 + 2 * inner :]
    gcxw[...] = sl[:taps]
    gcbw[...] = ss[:taps, :bc_width]
    gcxb[...] = sl[taps]
    ggn[...] = sl[taps + 1]
    gdtb[...] = sl[taps + 2, :heads]
    galog[...] = sl[taps + 3, :heads]
    gskip[...] = sl[taps + 4, :heads]
    gcbb[...] = ss[taps, :bc_width]
    gnorm_in[...] = ss[taps + 1]


def finish(g_own, d_normed, out_sum, small_loc, small_sh, hidden, cot, gate, vec, heads, bc_width,
           z0, inner, taps):
    rows, width = hidden.shape
    own = g_own.shape[0]

    def sds(*shape):
        return jax.ShapeDtypeStruct(shape, F32)

    outs = (
        jax.ShapeDtypeStruct((rows, width), BF16), sds(rows, width), sds(width), sds(own, inner),
        sds(own, inner), sds(own, bc_width), sds(own, heads), sds(taps, inner), sds(inner),
        sds(taps, bc_width), sds(bc_width), sds(heads), sds(heads), sds(heads), sds(inner),
        sds(own, inner),
    )
    results = pl.pallas_call(
        partial(finish_body, heads, bc_width, z0, inner, taps),
        out_shape=outs,
        in_specs=[VM] * 9,
        out_specs=(VM,) * 16,
        name="finish",
    )(g_own, d_normed, out_sum, small_loc, small_sh, hidden, cot, gate, vec)
    return (*results[:-1], results[-1].T)


def per_device(
    hidden_in, out_grad, segment_ids, norm_weight, w_z, w_x, w_bc, w_dt, conv_x_w, conv_x_b,
    conv_bc_w, conv_bc_b, dt_bias, a_log, d_skip, gnorm_weight, w_out,
):
    n, nt = lax.axis_size("dp"), lax.axis_size("tensor")
    rows_own, width = hidden_in.shape
    inner_loc = w_z.shape[1]
    inner_all = inner_loc * nt
    bc_width = w_bc.shape[1]
    heads = w_dt.shape[1]
    dt_pad = -(-heads // 128) * 128
    z0 = bc_width + dt_pad
    tokens = nt * rows_own
    head_dim = inner_loc // heads
    fused = (
        tokens == GROUP and inner_loc % 128 == 0 and 128 % head_dim == 0 and bc_width % 256 == 0
        and w_out.shape[1] <= 128
    )
    if fused:
        w_pack, vec, seg_col = prepare(
            w_z, w_x, w_bc, w_dt, w_out, segment_ids,
            (norm_weight, conv_x_b, gnorm_weight, conv_bc_b, dt_bias, a_log, d_skip), z0,
        )
    else:
        w_pack = jnp.concatenate([w_bc, pad_columns(w_dt, dt_pad), w_z, w_x, w_out.T], axis=1)
    w_all, hid_all, cot_all = gather_all(w_pack, hidden_in, out_grad)
    w_full = w_all.reshape(width, -1)
    w_cat = w_full[:, : z0 + 2 * inner_loc]
    w_out_t = w_full[:, z0 + 2 * inner_loc :]
    cot_all = cot_all.reshape(tokens, width)
    hid_all = hid_all.reshape(tokens, width)
    if fused:
        grads, dn_part, out_part, small_loc, small_sh, gate_all = fused_core(
            w_full, hid_all, cot_all, segment_ids, seg_col, conv_x_w, conv_bc_w, vec, heads,
            inner_loc, inner_all, bc_width, z0,
        )
        grads = grads.reshape(n, width // n, -1)
    else:
        hid_all = hid_all.astype(F32)
        rms_all = lax.rsqrt(jnp.mean(hid_all * hid_all, axis=1, keepdims=True) + epsilon)
        unit_all = hid_all * rms_all
        normed_all = (unit_all * norm_weight[None, :]).astype(BF16)
        projected_all = jnp.dot(normed_all, w_cat, preferred_element_type=F32)
        bc_proj = projected_all[:, :bc_width]
        dt_proj = projected_all[:, bc_width : bc_width + heads]
        z_proj = projected_all[:, z0 : z0 + inner_loc]
        x_proj = projected_all[:, z0 + inner_loc : z0 + 2 * inner_loc]
        back_proj = jnp.dot(cot_all, w_out_t, preferred_element_type=F32)
        core_fn = partial(mixer_core, segments=segment_ids[0], block_len=GROUP)
        gated, core_vjp = jax.vjp(
            core_fn, z_proj, x_proj, bc_proj, dt_proj, conv_x_w, conv_x_b, conv_bc_w, conv_bc_b,
            dt_bias, a_log, d_skip,
        )
        back_gated = back_proj * gated
        sums = tensor_sum(
            jnp.stack(
                [jnp.sum(gated * gated, axis=1), jnp.sum(back_gated * gnorm_weight[None, :], axis=1)]
            )
        )
        inv_gate = lax.rsqrt(sums[0] / inner_all + epsilon)
        cube_gate = inv_gate * inv_gate * inv_gate
        grad_gnorm = jnp.sum(inv_gate[:, None] * back_gated, axis=0)
        scaled_in = (gated * gnorm_weight[None, :]).astype(BF16)
        out_part = lax.dot_general(
            scaled_in, w_out_t, (((1,), (1,)), ((), ())), preferred_element_type=F32
        ).astype(BF16)
        d_gated = (inv_gate[:, None] * back_proj) * gnorm_weight[None, :] - (
            sums[1] * cube_gate / inner_all
        )[:, None] * gated
        scaled_out = (inv_gate[:, None] * scaled_in.astype(F32)).astype(BF16)
        core_grads = core_vjp(d_gated)
        d_z, d_x, d_bc, d_dt = [part.astype(BF16) for part in core_grads[:4]]
        d_proj = jnp.concatenate([d_bc, pad_columns(d_dt, dt_pad), d_z, d_x], axis=1)
        grad_wcat = lax.dot_general(
            normed_all, d_proj, (((0,), (0,)), ((), ())), preferred_element_type=F32
        ).astype(BF16)
        grad_wout_t = lax.dot_general(
            cot_all, scaled_out, (((0,), (0,)), ((), ())), preferred_element_type=F32
        ).astype(BF16)
        dn_part = lax.dot_general(
            d_proj, w_cat, (((1,), (1,)), ((), ())), preferred_element_type=F32
        )
        norm_part = jnp.sum(dn_part * unit_all, axis=0)
        grads = jnp.concatenate([grad_wcat, grad_wout_t], axis=1).reshape(n, width // n, -1)
        small_loc = jnp.concatenate(
            [
                core_grads[4],
                core_grads[5][None, :],
                grad_gnorm[None, :],
                *[pad_columns(core_grads[i][None, :], inner_loc) for i in (8, 9, 10)],
            ],
            axis=0,
        )
        small_sh = jnp.concatenate(
            [
                pad_columns(core_grads[6], width),
                pad_columns(core_grads[7][None, :], width),
                norm_part[None, :],
            ],
            axis=0,
        )
        dn_part, gate_all = dn_part.astype(BF16), inv_gate[:, None]
    g_own, d_normed, out_sum, small_loc, small_sh = reduce_all(
        grads,
        dn_part.reshape(nt, rows_own, width),
        out_part.reshape(nt, rows_own, width),
        small_loc,
        small_sh,
        bc_width,
    )
    taps = conv_x_w.shape[0]
    if fused:
        return finish(
            g_own, d_normed, out_sum, small_loc, small_sh, hidden_in, out_grad, gate_all, vec, heads,
            bc_width, z0, inner_loc, taps,
        )
    row_start = lax.axis_index("tensor") * rows_own
    hidden_f = hidden_in.astype(F32)
    inv_rms = lax.rsqrt(jnp.mean(hidden_f * hidden_f, axis=1, keepdims=True) + epsilon)
    gate_own = lax.dynamic_slice_in_dim(gate_all, row_start, rows_own, 0)
    block_out = (hidden_f + gate_own * out_sum).astype(BF16)
    d_scaled = d_normed * norm_weight[None, :]
    cube_rms = inv_rms * inv_rms * inv_rms
    grad_hidden = (
        out_grad.astype(F32)
        + inv_rms * d_scaled
        - cube_rms * hidden_f * jnp.mean(d_scaled * hidden_f, axis=1, keepdims=True)
    )
    taps = conv_x_w.shape[0]
    return (
        block_out,
        grad_hidden,
        small_sh[taps + 1],
        g_own[:, z0 : z0 + inner_loc],
        g_own[:, z0 + inner_loc : z0 + 2 * inner_loc],
        g_own[:, :bc_width],
        g_own[:, bc_width : bc_width + heads],
        small_loc[:taps],
        small_loc[taps],
        small_sh[:taps, :bc_width],
        small_sh[taps, :bc_width],
        small_loc[taps + 2, :heads],
        small_loc[taps + 3, :heads],
        small_loc[taps + 4, :heads],
        small_loc[taps + 1],
        g_own[:, z0 + 2 * inner_loc :].T,
    )


def solution(mesh):
    in_specs = (
        P(("dp", "tensor"), None),
        P(("dp", "tensor"), None),
        P("dp", None),
        P(),
        P("dp", "tensor"),
        P("dp", "tensor"),
        P("dp", None),
        P("dp", "tensor"),
        P(None, "tensor"),
        P("tensor"),
        P(),
        P(),
        P("tensor"),
        P("tensor"),
        P("tensor"),
        P("tensor"),
        P("tensor", "dp"),
    )
    out_specs = (
        P(("dp", "tensor"), None),
        P(("dp", "tensor"), None),
        P(),
        P("dp", "tensor"),
        P("dp", "tensor"),
        P("dp", None),
        P("dp", "tensor"),
        P(None, "tensor"),
        P("tensor"),
        P(),
        P(),
        P("tensor"),
        P("tensor"),
        P("tensor"),
        P("tensor"),
        P("tensor", "dp"),
    )
    return jax.shard_map(
        per_device, mesh=mesh, in_specs=in_specs, out_specs=out_specs, check_vma=False
    )
```

profile of v0, /device:TPU:0, one launch (start us, length us, event | category | flops | bytes accessed | tf_op | source)
XLA Modules:
  0.0 113.4 jit_solution(9038223763663818900)
XLA Ops:
  0.6 1.4 %copy.33.wdt = bf16[48,12]{1,0:T(8,128)(2,1)} copy(bf16[48,12]{0,1:T(8,128)(2,1)} %param.24) | data formatting | bytes 2304 | tf_op args[7]
  2.0 1.8 %prepare.1 = (bf16[48,2688]{1,0:T(8,128)(2,1)}, f32[8,768]{1,0:T(8,128)}, f32[256,128]{1,0:T(8,128)}) custom-call(bf16[48,768]{1,0:T(8,128)(2,1)} %wz.1, bf16[48,768]{1,0:T(8,128)(2,1)} %wx.1, bf16[48,256]{1,0:T(8,128)(2,1)} %wbc.1, bf16[48,12]{1,0:T(8,128)(2,1)} %copy.33.wdt, bf16[48,768]{1,0:T(8,128)(2,1)} %bitcast.17, s32[1,256]{1,0:T(1,128)} %segr.3, ...), custom_call_target="tpu_custom_call" | custom-call | tf_op jit(solution)/shard_map/prepare/pallas_call | solution.py:729
  3.9 35.1 %gather_all.1 = (bf16[16,48,2688]{2,1,0:T(8,128)(2,1)}, bf16[2,128,768]{2,1,0:T(8,128)(2,1)}, bf16[2,128,768]{2,1,0:T(8,128)(2,1)}) custom-call(bf16[48,2688]{1,0:T(8,128)(2,1)} %get-tuple-element.54.w_ref, bf16[128,768]{1,0:T(8,128)(2,1)} %hidden.1, bf16[128,768]{1,0:T(8,128)(2,1)} %cot.1), custom_call_target="tpu_custom_call" | custom-call | tf_op jit(solution)/shard_map/gather_all/pallas_call | solution.py:261
  39.0 6.7 %core_fwd.1 = (f32[256,1920]{1,0:T(8,128)}, f32[256,768]{1,0:T(8,128)}, f32[256,768]{1,0:T(8,128)}, bf16[256,768]{1,0:T(8,128)(2,1)}, f32[8,256]{1,0:T(8,128)}) custom-call(bf16[768,2688]{1,0:T(8,128)(2,1)} %bitcast.8, bf16[256,768]{1,0:T(8,128)(2,1)} %bitcast.11, bf16[256,768]{1,0:T(8,128)(2,1)} %bitcast.13, f32[256,128]{1,0:T(8,128)} %get-tuple-element.58.segc_ref, ...), custom_call_target="tpu_custom_call" | custom-call | tf_op jit(solution)/shard_map/core_fwd/pallas_call | solution.py:752
  45.7 5.0 %tensor_sum.1.sum_ref = f32[8,256]{1,0:T(8,128)} custom-call(f32[8,256]{1,0:T(8,128)} %get-tuple-element.64.p_ref), custom_call_target="tpu_custom_call" | custom-call | tf_op jit(solution)/shard_map/tensor_sum/pallas_call | solution.py:303
  50.7 12.8 %core_bwd.1 = (bf16[768,2688]{1,0:T(8,128)(2,1)}, bf16[256,768]{1,0:T(8,128)(2,1)}, bf16[256,768]{1,0:T(8,128)(2,1)}, f32[9,768]{1,0:T(8,128)}, f32[6,768]{1,0:T(8,128)}, /*index=5*/f32[256,128]{1,0:T(8,128)}) custom-call(bf16[768,2688]{1,0:T(8,128)(2,1)} %bitcast.9, bf16[256,768]{1,0:T(8,128)(2,1)} %bitcast.12, bf16[256,768]{1,0:T(8,128)(2,1)} %bitcast.14, ...), custom_call_target="tpu_custom_call" | custom-call | tf_op jit(solution)/shard_map/core_bwd/pallas_call | solution.py:761
  63.6 45.7 %reduce_all.1 = (f32[48,2688]{1,0:T(8,128)}, f32[128,768]{1,0:T(8,128)}, f32[128,768]{1,0:T(8,128)}, f32[9,768]{1,0:T(8,128)}, f32[6,768]{1,0:T(8,128)}) custom-call(bf16[16,48,2688]{2,1,0:T(8,128)(2,1)} %bitcast.10, bf16[2,128,768]{2,1,0:T(8,128)(2,1)} %bitcast.15, bf16[2,128,768]{2,1,0:T(8,128)(2,1)} %bitcast.16, f32[9,768]{1,0:T(8,128)} %get-tuple-element.68.sl_ref, ...), custom_call_target="tpu_custom_call" | custom-call | tf_op jit(solution)/shard_map/reduce_all/pallas_call | solution.py:454
  109.3 2.7 %finish.1 = (bf16[128,768]{1,0:T(8,128)(2,1)}, f32[128,768]{1,0:T(8,128)}, f32[768]{0:T(1024)}, f32[48,768]{1,0:T(8,128)}, f32[48,768]{1,0:T(8,128)}, /*index=5*...) custom-call(f32[48,2688]{1,0:T(8,128)} %get-tuple-element.70.g, ...), custom_call_target="tpu_custom_call" | custom-call | tf_op jit(solution)/shard_map/finish/pallas_call | solution.py:818
  112.0 1.4 %copy.34 = f32[48,12]{0,1:T(8,128)} copy(f32[48,12]{1,0:T(8,128)} %get-tuple-element.98) | data formatting | bytes 4608
where the time goes:
time: 114 us; the launch traced here: 113 us
  Pallas kernels  110 us (96%)
  local copies, waits for them, and re-layouts  2.79 us (2%)
    pallas_call x1, Pallas kernels, reduce_all(): pl.pallas_call(partial(reduce_body, n, nt, bc_width), out_shape=(jax.Shap...  45.7 us
    pallas_call x1, Pallas kernels, gather_all(): pl.pallas_call(partial(gather_body, n, nt), out_shape=(jax.ShapeDtypeStru...  35.1 us
    pallas_call x1, Pallas kernels, fused_core(): pl.pallas_call(partial(core_bwd_body, heads, inner, inner_all, bc_width,...  12.8 us
    pallas_call x1, Pallas kernels, fused_core(): pl.pallas_call(partial(core_fwd_body, heads, inner, bc_width, z0), out_sh...  6.74 us
    pallas_call x1, Pallas kernels, tensor_sum(): pl.pallas_call(partial(pair_body, nt), out_shape=jax.ShapeDtypeStruct(val...  4.98 us
    unnamed x2, local copies, waits for them, and re-layouts  2.79 us
    pallas_call x1, Pallas kernels, finish(): pl.pallas_call(partial(finish_body, heads, bc_width, z0, inner, taps), ou...  2.71 us

commit v1 on v0

--- a/solution.py
+++ b/solution.py
@@ -532,121 +532,347 @@
     return jnp.where(channel // head_dim == head, 1.0, 0.0)
 
 
-def scan_setup(p_ref, seg_col, seg_row, cxw, cxb, cbw, cbb, dtb, alog, z0, bc_width, inner):
-    masks = conv_masks(seg_col, cxw.shape[0])
-    length = seg_col.shape[0]
-    x_raw = p_ref[:, z0 + inner : z0 + 2 * inner]
-    bc_raw = p_ref[:, :bc_width]
-    x_pre = conv_pre(x_raw, cxw, cxb, masks)
-    bc_pre = conv_pre(bc_raw, cbw, cbb, masks)
-    u = p_ref[:, bc_width:z0] + dtb
-    step = jnp.maximum(u, 0.0) + jnp.log1p(jnp.exp(-jnp.abs(u)))
-    rate = -jnp.exp(alog)
-    log_decay = rate * step
+def prepare_body(bc_width, wbc, wdt, seg, nw, cxb, gnw, cbb, dtb, alog, dskip, pack, vec, segc):
+    lanes = pack.shape[1] - bc_width
+    heads = wdt.shape[0]
+    head = lax.broadcasted_iota(jnp.int32, (heads, lanes), 0)
+    lane = lax.broadcasted_iota(jnp.int32, (heads, lanes), 1)
+    unit = jnp.where(head == lane, 1.0, 0.0).astype(BF16)
+    pack[:, :bc_width] = wbc[...]
+    pack[:, bc_width:] = mm(wdt[...], unit, ((0,), (0,))).astype(BF16)
+    vec[...] = jnp.zeros(vec.shape, F32)
+    for i, ref in enumerate((nw, cxb, gnw, cbb, dtb, alog, dskip)):
+        vec[i : i + 1, : ref.shape[0]] = ref[...][None, :]
+    segc[...] = jnp.broadcast_to(seg[...].astype(F32), (128, seg.shape[1])).T
+
+
+def prepare(w_bc, w_dt, segments, vectors, lanes):
+    rows, bc_width = w_bc.shape
+    width = max(v.shape[0] for v in vectors)
+    length = segments.shape[1]
+    return pl.pallas_call(
+        partial(prepare_body, bc_width),
+        out_shape=(
+            jax.ShapeDtypeStruct((rows, bc_width + lanes), BF16),
+            jax.ShapeDtypeStruct((8, width), F32),
+            jax.ShapeDtypeStruct((length, 128), F32),
+        ),
+        in_specs=[VM] * 10,
+        out_specs=(VM,) * 3,
+        name="prepare",
+    )(w_bc, w_dt.T, segments, *vectors)
+
+
+def mega_body(n, nt, heads, inner_all, bc_width, *refs):
+    (wbd, wx, wz, wo, h_ref, o_ref, segc_ref, segr, cxw, cbw, vec,
+     gbd_out, gx_out, gz_out, go_out, dn_out, op_out, sl_out, ss_out, gate_out,
+     abd, ax, az, ao, h_all, o_all,
+     bdraw, xraw, xpre_s, dsil_s, xconv_s, stepw_s, xstep_s, bcpre_s, bcconv_s, u_s, step_s, cum_s,
+     scores_s, decay_s, y_s, back_s, zsil_s, zdsil_s, gated_s, scaled_s, sum_t, norm_s,
+     dy_s, dx_s, dz_b, dx_b, dbd_b,
+     g_bd, g_x, g_z, g_o, cg_bd, cg_x, cg_z, cg_o, xp_bd, xp_x, xp_z, xp_o, xg_bd, xg_x, xg_z, xg_o,
+     zp_bd, zp_x, zp_z, zp_o, zg_bd, zg_x, zg_z, zg_o,
+     op_s, dn_s, op_got, dn_got, bc_put, bc_got,
+     sl_s, ss_s, sl_c, sl_xput, sl_x, sl_z, ss_t, ss_cput, ss_c, ss_xput, ss_x, ss_z,
+     azs, azr, axs, axr, acs, acr, ys, yr, rcs, rcr, rxs, rxr, rzs, rzr, scs, scr, sxs, sxr, szs, szr) = refs
+    me, z, x, c = place(n)
+    t = lax.axis_index("tensor")
+    zn = n // 4
+    rows = wx.shape[0]
+    width = h_ref.shape[1]
+    inner = wx.shape[1]
+    own_rows = h_ref.shape[0]
+    lanes = wbd.shape[1] - bc_width
+    head_dim = inner // heads
+    state = bc_width // 2
+    length = nt * own_rows
+    taps = cxw.shape[0]
+    z_peer, x_peer, c_peer, t_peer = peers_of(n, nt)
+    above, below = z_peer[1], z_peer[zn - 1]
+    has_above, has_below = z < zn - 1, z > 0
+    greet(list(z_peer.values()) + [x_peer, c_peer] + list(t_peer.values()))
+    started = []
+
+    def go(src, dst, send_sem, recv_sem, peer):
+        copy = remote(src, dst, send_sem, recv_sem, peer)
+        copy.start()
+        started.append(copy)
+
+    def arrived(dst, send_sem, recv_sem, peer):
+        remote(dst, dst, send_sem, recv_sem, peer).wait_recv()
+
+    BD, X, Z, O = range(4)
+    own = (wbd, wx, wz, wo)
+    full = (abd, ax, az, ao)
+
+    def slot(level, side, core):
+        return pl.ds(pl.multiple_of((level * 4 + side * 2 + core) * rows, 16), rows)
+
+    def z_go(src, dst, ti, level, up):
+        remote(src, dst, azs.at[(2 * ti + (0 if up else 1)) * zn + level], azr.at[ti * zn + level],
+               above if up else below).start()
+
+    def x_go(src, dst, ti, level):
+        remote(src, dst, axs.at[ti * zn + level], axr.at[ti * zn + level], x_peer).start()
+
+    def c_go(src, dst, ti, half, level):
+        j = (2 * ti + half) * zn + level
+        remote(src, dst, acs.at[j], acr.at[j], c_peer).start()
+
+    def send_own(ti):
+        src, dst = own[ti], full[ti].at[slot(z, x, c)]
+
+        @pl.when(has_above)
+        def _():
+            z_go(src, dst, ti, z, True)
+
+        @pl.when(has_below)
+        def _():
+            z_go(src, dst, ti, z, False)
+
+        x_go(src, dst, ti, z)
+        c_go(src, dst, ti, 0, z)
+        full[ti][slot(z, x, c), :] = src[...]
+
+    def by_distance(s, visit):
+        @pl.when(z - s >= 0)
+        def _():
+            visit(z - s, True)
+
+        @pl.when(z + s < zn)
+        def _():
+            visit(z + s, False)
+
+    def take(ti, s):
+        def visit(level, up):
+            got = full[ti].at[slot(level, x, c)]
+            arrived(got, azs.at[2 * ti * zn + level], azr.at[ti * zn + level], above)
+
+            @pl.when(has_above if up else has_below)
+            def _():
+                z_go(got, got, ti, level, up)
+
+            x_go(got, got, ti, level)
+            c_go(got, got, ti, 0, level)
+
+        by_distance(s, visit)
+
+    def cross(ti, s):
+        def visit(level, up):
+            got = full[ti].at[slot(level, 1 - x, c)]
+            arrived(got, axs.at[ti * zn + level], axr.at[ti * zn + level], x_peer)
+            c_go(got, got, ti, 1, level)
+
+        if s == 0:
+            visit(z, True)
+        else:
+            by_distance(s, visit)
+
+    def complete(ti):
+        for half in range(2):
+            side = x if half == 0 else 1 - x
+            for level in range(zn):
+                j = (2 * ti + half) * zn + level
+                arrived(full[ti].at[slot(level, side, 1 - c)], acs.at[j], acr.at[j], c_peer)
+
+    def y_go(kind, src, dst, k):
+        go(src, dst, ys.at[kind * nt + k], yr.at[kind * nt + k], t_peer[k])
+
+    def y_got(kind, dst, k):
+        arrived(dst, ys.at[kind * nt + k], yr.at[kind * nt + k], t_peer[k])
+
+    def token_rows(i):
+        return pl.ds(pl.multiple_of(i * own_rows, 16), own_rows)
+
+    send_own(BD)
+    send_own(X)
+    for k in range(1, nt):
+        y_go(0, h_ref, h_all.at[token_rows(t)], k)
+        y_go(1, o_ref, o_all.at[token_rows(t)], k)
+    send_own(Z)
+    h_all[token_rows(t), :] = h_ref[...]
+    o_all[token_rows(t), :] = o_ref[...]
+    take(BD, 1)
+    take(X, 1)
+    send_own(O)
+    segc = segc_ref[:, :1]
+    nw, cxb, gnw = vec[0:1, :width], vec[1:2, :inner], vec[2:3, :inner]
+    cbb, dtb = vec[3:4, :bc_width], vec[4:5, :lanes]
+    alog, dskip = vec[5:6, :lanes], vec[6:7, :lanes]
+    for k in range(1, nt):
+        y_got(0, h_all.at[token_rows((t + nt - k) % nt)], k)
+    hid = h_all[...].astype(F32)
+    rms = lax.rsqrt(jnp.mean(hid * hid, axis=1, keepdims=True) + epsilon)
+    norm_s[...] = (hid * rms * nw).astype(BF16)
+    cross(BD, 0)
+    cross(X, 0)
+    for s in range(2, zn):
+        take(BD, s)
+        take(X, s)
+        take(Z, s - 1)
+    take(O, 1)
+    for s in range(1, zn):
+        cross(BD, s)
+        cross(X, s)
+        if s == 1:
+            cross(Z, 0)
+            cross(O, 0)
+    if zn > 2:
+        take(O, 2)
+    take(Z, zn - 1)
+    complete(BD)
+    complete(X)
+
+    masks = conv_masks(segc, taps)
     row = lax.broadcasted_iota(jnp.int32, (length, length), 0)
     col = lax.broadcasted_iota(jnp.int32, (length, length), 1)
-    lower = jnp.where(row >= col, 1.0, 0.0)
-    cum = mm(lower, log_decay, precision=HIGH)
-    allowed = (row >= col) & (seg_col == seg_row)
-    return masks, x_raw, bc_raw, x_pre, bc_pre, u, step, rate, cum, allowed, row, col
-
-
-def core_fwd_body(heads, inner, bc_width, z0, w_ref, hid_ref, cot_ref, segc_ref, segr, cxw, cbw, vec,
-                  p_out, y_out, back_out, norm_out, sum_out):
-    nw, cxb, gnw = vec[0:1, : hid_ref.shape[1]], vec[1:2, :inner], vec[2:3, :inner]
-    cbb, dtb = vec[3:4, :bc_width], vec[4:5, : z0 - bc_width]
-    alog, dskip = vec[5:6, : z0 - bc_width], vec[6:7, : z0 - bc_width]
-    segc = segc_ref[:, :1]
-    head_dim = inner // heads
-    hid = hid_ref[...].astype(F32)
-    rms = lax.rsqrt(jnp.mean(hid * hid, axis=1, keepdims=True) + epsilon)
-    norm_out[...] = (hid * rms * nw).astype(BF16)
-    p_out[...] = mm(norm_out[...], w_ref[:, : z0 + 2 * inner])
-    back_out[...] = mm(cot_ref[...], w_ref[:, z0 + 2 * inner :])
-    (_, _, _, x_pre, bc_pre, _, step, _, cum, allowed, _, _) = scan_setup(
-        p_out, segc, segr[...].astype(F32), cxw[...], cxb, cbw[...], cbb, dtb, alog,
-        z0, bc_width, inner)
-    spread = head_map(step.shape[1], inner, head_dim)
-    x_conv = x_pre * sigmoid(x_pre)
+    allowed = (row >= col) & (segc == segr[...].astype(F32))
+    bdraw[...] = mm(norm_s[...], abd[...])
+    xraw[...] = mm(norm_s[...], ax[...])
+    bc_pre = conv_pre(bdraw[:, :bc_width], cbw[...], cbb, masks)
+    bcpre_s[...] = bc_pre
     bc_conv = (bc_pre * sigmoid(bc_pre)).astype(BF16)
-    state = bc_width // 2
-    scores = mm(bc_conv[:, state:], bc_conv[:, :state], ((1,), (1,)))
-    scores = jnp.where(allowed, scores, 0.0)
-    x_step = (x_conv * mm(step, spread, precision=HIGH)).astype(BF16)
-    skip = mm(jnp.broadcast_to(dskip, (8, step.shape[1])), spread, precision=HIGH)[:1]
+    bcconv_s[...] = bc_conv
+    u = bdraw[:, bc_width:] + dtb
+    step = jnp.maximum(u, 0.0) + jnp.log1p(jnp.exp(-jnp.abs(u)))
+    u_s[...] = u
+    step_s[...] = step
+    rate = -jnp.exp(alog)
+    cum_s[...] = mm(jnp.where(row >= col, 1.0, 0.0), rate * step, precision=HIGH)
+    x_pre = conv_pre(xraw[...], cxw[...], cxb, masks)
+    x_sig = sigmoid(x_pre)
+    dsil_s[...] = x_sig * (1.0 + x_pre * (1.0 - x_sig))
+    xconv_s[...] = x_pre * x_sig
+    spread = head_map(lanes, inner, head_dim)
+    stepw_s[...] = mm(step, spread, precision=HIGH)
+    xstep_s[...] = (xconv_s[...] * stepw_s[...]).astype(BF16)
+    skip = mm(jnp.broadcast_to(dskip, (8, lanes)), spread, precision=HIGH)[:1]
+    scores_s[...] = jnp.where(allowed, mm(bc_conv[:, state:], bc_conv[:, :state], ((1,), (1,))), 0.0)
+    for s in range(3, zn):
+        take(O, s)
+    cross(Z, 1)
+    per = 128 // head_dim
+    lane = lax.broadcasted_iota(jnp.int32, (length, 128), 1)
+    groups = heads // per
+    relays = [partial(cross, O, 1)]
+    for s in range(2, zn):
+        relays += [partial(cross, Z, s), partial(cross, O, s)]
+    cum = cum_s[...]
     cum_t = cum.T
-    per = 128 // head_dim
-    for g in range(heads // per):
+    for g in range(groups):
         cols = slice(g * 128, (g + 1) * 128)
-        lane = lax.broadcasted_iota(jnp.int32, (x_step.shape[0], 128), 1)
         part = None
         for i in range(per):
             h = g * per + i
             decay = jnp.exp(jnp.where(allowed, cum[:, h : h + 1] - cum_t[h : h + 1, :], 0.0))
-            one = mm((decay * scores).astype(BF16), x_step[:, cols])
+            decay_s[h] = decay
+            one = mm((decay * scores_s[...]).astype(BF16), xstep_s[:, cols])
             part = one if part is None else jnp.where(lane < i * head_dim, part, one)
-        y_out[:, cols] = part + skip[:, cols] * x_conv[:, cols]
-    z = p_out[:, z0 : z0 + inner]
-    gated = y_out[...] * (z * sigmoid(z))
+        y_s[:, cols] = part + skip[:, cols] * xconv_s[:, cols]
+        if relays:
+            relays.pop(0)()
+    for relay in relays:
+        relay()
+    complete(Z)
+    z_val = mm(norm_s[...], az[...])
+    z_sig = sigmoid(z_val)
+    zsil_s[...] = z_val * z_sig
+    zdsil_s[...] = z_sig * (1.0 + z_val * (1.0 - z_sig))
+    gated = y_s[...] * zsil_s[...]
+    gated_s[...] = gated
+    scaled_s[...] = (gated * gnw).astype(BF16)
     sq = jnp.sum(gated * gated, axis=1, keepdims=True)
-    dot = jnp.sum(back_out[...] * gated * gnw, axis=1, keepdims=True)
-    lane = lax.broadcasted_iota(jnp.int32, (gated.shape[0], 128), 1)
+    for k in range(1, nt):
+        y_got(1, o_all.at[token_rows((t + nt - k) % nt)], k)
+    complete(O)
+    back_s[...] = mm(o_all[...], ao[...])
+    dot = jnp.sum(back_s[...] * gated_s[...] * gnw, axis=1, keepdims=True)
     both = jnp.where(lane == 0, sq, jnp.where(lane == 1, dot, 0.0))
-    sum_out[...] = both.T[:8]
-
-
-def core_bwd_body(heads, inner, inner_all, bc_width, z0, w_ref, hid_ref, cot_ref, segc_ref, segr, cxw, cbw, vec, p_ref, y_ref, back_ref, norm_ref, sum_ref,
-                  grad_out, dn_out, op_out, loc_out, sh_out, gate_out, dy_s, dx_s, dproj_s):
-    nw, cxb, gnw = vec[0:1, : hid_ref.shape[1]], vec[1:2, :inner], vec[2:3, :inner]
-    cbb, dtb = vec[3:4, :bc_width], vec[4:5, : z0 - bc_width]
-    alog, dskip = vec[5:6, : z0 - bc_width], vec[6:7, : z0 - bc_width]
-    segc = segc_ref[:, :1]
-    head_dim = inner // heads
-    state = bc_width // 2
-    length = segc.shape[0]
-    taps = cxw.shape[0]
-    sums = jnp.concatenate([sum_ref[...], jnp.zeros((120, length), F32)], axis=0).T
+    sum_t[pl.ds(t, 1)] = both.T[:8][None]
+    for k in range(1, nt):
+        y_go(2, sum_t.at[t], sum_t.at[t], k)
+    op_s[...] = mm(scaled_s[...], ao[...], ((1,), (1,))).astype(BF16)
+    for k in range(1, nt):
+        y_go(3, op_s.at[token_rows((t + k) % nt)], op_got.at[t], k)
+    sl_s[...] = jnp.zeros(sl_s.shape, F32)
+    ss_s[...] = jnp.zeros(ss_s.shape, F32)
+    for k in range(1, nt):
+        y_got(2, sum_t.at[(t + nt - k) % nt], k)
+    total = sum_t[0]
+    for i in range(1, nt):
+        total = total + sum_t[i]
+    sums = jnp.concatenate([total, jnp.zeros((120, length), F32)], axis=0).T
     inv = lax.rsqrt(sums[:, :1] / inner_all + epsilon)
     gate_out[...] = jnp.broadcast_to(inv, (length, 128))
     coef = sums[:, 1:2] * (inv * inv * inv) / inner_all
-    z = p_ref[:, z0 : z0 + inner]
-    z_sig = sigmoid(z)
-    z_silu = z * z_sig
-    y = y_ref[...]
-    gated = y * z_silu
-    grad_q = inv * back_ref[...]
-    loc_out[...] = jnp.zeros(loc_out.shape, F32)
-    sh_out[...] = jnp.zeros(sh_out.shape, F32)
-    loc_out[taps + 1 : taps + 2, :] = jnp.sum(grad_q * gated, axis=0, keepdims=True)
-    scaled = (gated * gnw).astype(BF16)
-    op_out[...] = mm(scaled, w_ref[:, z0 + 2 * inner :], ((1,), (1,))).astype(BF16)
-    scaled_out = (inv * scaled.astype(F32)).astype(BF16)
-    grad_out[:, z0 + 2 * inner :] = mm(cot_ref[...], scaled_out, ((0,), (0,))).astype(BF16)
-    d_gated = grad_q * gnw - coef * gated
-    dy_s[...] = d_gated * z_silu
-    dproj_s[:, z0 : z0 + inner] = (d_gated * y * (z_sig * (1.0 + z * (1.0 - z_sig)))).astype(BF16)
-
-    (masks, x_raw, bc_raw, x_pre, bc_pre, u, step, rate, cum, allowed, row, col) = scan_setup(
-        p_ref, segc, segr[...].astype(F32), cxw[...], cxb, cbw[...], cbb, dtb, alog,
-        z0, bc_width, inner)
-    lanes = step.shape[1]
-    spread = head_map(lanes, inner, head_dim)
-    x_sig = sigmoid(x_pre)
-    x_conv = x_pre * x_sig
-    bc_sig = sigmoid(bc_pre)
-    bc_conv = (bc_pre * bc_sig).astype(BF16)
-    b_state, c_state = bc_conv[:, :state], bc_conv[:, state:]
-    scores = jnp.where(allowed, mm(c_state, b_state, ((1,), (1,))), 0.0)
-    step_wide = mm(step, spread, precision=HIGH)
-    x_step = (x_conv * step_wide).astype(BF16)
-    skip = mm(jnp.broadcast_to(dskip, (8, lanes)), spread, precision=HIGH)[:1]
-    cum_t = cum.T
-    per = 128 // head_dim
-    lane = lax.broadcasted_iota(jnp.int32, (length, 128), 1)
+
+    grad = (g_bd, g_x, g_z, g_o)
+    cgot = (cg_bd, cg_x, cg_z, cg_o)
+    xput = (xp_bd, xp_x, xp_z, xp_o)
+    xgot = (xg_bd, xg_x, xg_z, xg_o)
+    zput = (zp_bd, zp_x, zp_z, zp_o)
+    zgot = (zg_bd, zg_x, zg_z, zg_o)
+    gout = (gbd_out, gx_out, gz_out, go_out)
+    order = ring_order(zn)
+    order = order[2:] + order[:2]
+    zorder = order + [0]
+
+    def mine(k, side, core):
+        return slot((z + k) % zn, side, core)
+
+    def c_send(ti):
+        for half in range(2):
+            side = 1 - x if half == 0 else x
+            for k in zorder:
+                j = half * zn + k
+                go(grad[ti].at[mine(k, side, 1 - c)], cgot[ti].at[j], rcs.at[2 * zn * ti + j],
+                   rcr.at[2 * zn * ti + j], c_peer)
+
+    def x_send(ti, k):
+        j = 2 * zn * ti + k
+        arrived(cgot[ti].at[k], rcs.at[j], rcr.at[j], c_peer)
+        part = grad[ti][mine(k, 1 - x, c), :].astype(F32) + cgot[ti][k].astype(F32)
+        xput[ti][k] = part.astype(BF16)
+        go(xput[ti].at[k], xgot[ti].at[k], rxs.at[zn * ti + k], rxr.at[zn * ti + k], x_peer)
+
+    def z_send(ti, k):
+        j = 2 * zn * ti + zn + k
+        arrived(cgot[ti].at[zn + k], rcs.at[j], rcr.at[j], c_peer)
+        part = grad[ti][mine(k, x, c), :].astype(F32) + cgot[ti][zn + k].astype(F32)
+        arrived(xgot[ti].at[k], rxs.at[zn * ti + k], rxr.at[zn * ti + k], x_peer)
+        part = part + xgot[ti][k].astype(F32)
+        if k == 0:
+            gout[ti][...] = part
+        else:
+            zput[ti][k] = part.astype(BF16)
+            go(zput[ti].at[k], zgot[ti].at[k], rzs.at[zn * ti + k], rzr.at[zn * ti + k], z_peer[k])
+
+    def z_done(ti):
+        part = gout[ti][...]
+        for k in order:
+            arrived(zgot[ti].at[k], rzs.at[zn * ti + k], rzr.at[zn * ti + k], z_peer[k])
+            part = part + zgot[ti][k].astype(F32)
+        gout[ti][...] = part
+
+    scaled_out = (inv * scaled_s[...].astype(F32)).astype(BF16)
+    g_o[...] = mm(o_all[...], scaled_out, ((0,), (0,))).astype(BF16)
+    c_send(O)
+    grad_q = inv * back_s[...]
+    sl_s[taps + 1 : taps + 2, :] = jnp.sum(grad_q * gated_s[...], axis=0, keepdims=True)
+    d_gated = grad_q * gnw - coef * gated_s[...]
+    dy_s[...] = d_gated * zsil_s[...]
+    dz_b[...] = (d_gated * y_s[...] * zdsil_s[...]).astype(BF16)
+    for k in zorder:
+        x_send(O, k)
+    g_z[...] = mm(norm_s[...], dz_b[...], ((0,), (0,))).astype(BF16)
+    c_send(Z)
+    relays = [lambda: [x_send(Z, k) for k in zorder]]
+    relays += [partial(z_send, O, k) for k in zorder]
+
     d_scores = jnp.zeros((length, length), F32)
     row_sums = jnp.zeros((length, 128), F32)
     col_sums = []
-    for g in range(heads // per):
+    for g in range(groups):
         cols = slice(g * 128, (g + 1) * 128)
         dy = dy_s[:, cols]
         dy_b = dy.astype(BF16)
@@ -654,10 +880,9 @@
         for i in range(per):
             h = g * per + i
             inside = (lane >= i * head_dim) & (lane < (i + 1) * head_dim)
-            decay = jnp.where(
-                allowed, jnp.exp(jnp.where(allowed, cum[:, h : h + 1] - cum_t[h : h + 1, :], 0.0)), 0.0)
-            weight = decay * scores
-            d_weight = mm(jnp.where(inside, dy, 0.0).astype(BF16), x_step[:, cols], ((1,), (1,)))
+            decay = decay_s[h]
+            weight = decay * scores_s[...]
+            d_weight = mm(jnp.where(inside, dy, 0.0).astype(BF16), xstep_s[:, cols], ((1,), (1,)))
             d_scores = d_scores + d_weight * decay
             flow = d_weight * weight
             row_sums = jnp.where(lane == h, jnp.sum(flow, axis=1, keepdims=True), row_sums)
@@ -665,112 +890,213 @@
             one = mm(weight.astype(BF16), dy_b, ((0,), (0,)))
             part = one if part is None else jnp.where(lane < i * head_dim, part, one)
         dx_s[:, cols] = part
+        if relays:
+            relays.pop(0)()
+    for relay in relays:
+        relay()
     col_rows = jnp.concatenate(col_sums + [jnp.zeros((128 - heads, length), F32)], axis=0)
     d_cum = row_sums - col_rows.T
+    row = lax.broadcasted_iota(jnp.int32, (length, length), 0)
+    col = lax.broadcasted_iota(jnp.int32, (length, length), 1)
+    allowed = (row >= col) & (segc == segr[...].astype(F32))
     d_log = mm(jnp.where(row <= col, 1.0, 0.0), d_cum, precision=HIGH)
-    d_xs = dx_s[...]
+    spread = head_map(lanes, inner, head_dim)
+    d_step = mm((dx_s[...] * xconv_s[...]).astype(BF16), spread.astype(BF16), ((1,), (1,)))
+    rate = -jnp.exp(alog)
+    d_step = d_step + rate * d_log
+    d_u = d_step * sigmoid(u_s[...])
+    head_lane = lax.broadcasted_iota(jnp.int32, (length, lanes), 1)
+    dbd_b[:, bc_width:] = jnp.where(head_lane < heads, d_u, 0.0).astype(BF16)
+    masks = conv_masks(segc, taps)
+    d_scores = jnp.where(allowed, d_scores, 0.0).astype(BF16)
+    d_b = mm(d_scores, bcconv_s[:, state:], ((0,), (0,)))
+    d_c = mm(d_scores, bcconv_s[:, :state])
+    bc_pre = bcpre_s[...]
+    bc_sig = sigmoid(bc_pre)
+    d_bcpre = jnp.concatenate([d_b, d_c], axis=1) * (bc_sig * (1.0 + bc_pre * (1.0 - bc_sig)))
+    d_bc, conv_rows, bias_row = conv_back(d_bcpre, bdraw[:, :bc_width], cbw[...], masks)
+    dbd_b[:, :bc_width] = d_bc.astype(BF16)
+    for k in range(taps):
+        ss_s[k : k + 1, :bc_width] = conv_rows[k]
+    ss_s[taps : taps + 1, :bc_width] = bias_row
+    g_bd[...] = mm(norm_s[...], dbd_b[...], ((0,), (0,))).astype(BF16)
+    c_send(BD)
+
     dy = dy_s[...]
-    d_step = mm((d_xs * x_conv).astype(BF16), spread.astype(BF16), ((1,), (1,)))
-    d_step = d_step + rate * d_log
-    d_u = d_step * sigmoid(u)
-    skip_row = jnp.sum(dy * x_conv, axis=0, keepdims=True)
+    skip = mm(jnp.broadcast_to(dskip, (8, lanes)), spread, precision=HIGH)[:1]
+    d_xpre = (dx_s[...] * stepw_s[...] + skip * dy) * dsil_s[...]
+    d_x, conv_rows, bias_row = conv_back(d_xpre, xraw[...], cxw[...], masks)
+    dx_b[...] = d_x.astype(BF16)
+    for k in range(taps):
+        sl_s[k : k + 1, :] = conv_rows[k]
+    sl_s[taps : taps + 1, :] = bias_row
+    for k in zorder:
+        x_send(BD, k)
+    g_x[...] = mm(norm_s[...], dx_b[...], ((0,), (0,))).astype(BF16)
+    c_send(X)
+    skip_row = jnp.sum(dy * xconv_s[...], axis=0, keepdims=True)
     d_skip = mm(jnp.broadcast_to(skip_row, (8, inner)), spread, ((1,), (1,)), precision=HIGH)[:1]
-    loc_out[taps + 2 : taps + 3, :lanes] = jnp.sum(d_u, axis=0, keepdims=True)
-    loc_out[taps + 3 : taps + 4, :lanes] = rate * jnp.sum(d_log * step, axis=0, keepdims=True)
-    loc_out[taps + 4 : taps + 5, :lanes] = d_skip
-    head_lane = lax.broadcasted_iota(jnp.int32, (length, lanes), 1)
-    dproj_s[:, bc_width:z0] = jnp.where(head_lane < heads, d_u, 0.0).astype(BF16)
-
-    d_xpre = (d_xs * step_wide + skip * dy) * (x_sig * (1.0 + x_pre * (1.0 - x_sig)))
-    d_x, rows, bias_row = conv_back(d_xpre, x_raw, cxw[...], masks)
-    dproj_s[:, z0 + inner : z0 + 2 * inner] = d_x.astype(BF16)
-    for k in range(taps):
-        loc_out[k : k + 1, :] = rows[k]
-    loc_out[taps : taps + 1, :] = bias_row
-
-    d_scores = d_scores.astype(BF16)
-    d_b = mm(d_scores, c_state, ((0,), (0,)))
-    d_c = mm(d_scores, b_state)
-    d_bcpre = jnp.concatenate([d_b, d_c], axis=1) * (bc_sig * (1.0 + bc_pre * (1.0 - bc_sig)))
-    d_bc, rows, bias_row = conv_back(d_bcpre, bc_raw, cbw[...], masks)
-    dproj_s[:, :bc_width] = d_bc.astype(BF16)
-    for k in range(taps):
-        sh_out[k : k + 1, :bc_width] = rows[k]
-    sh_out[taps : taps + 1, :bc_width] = bias_row
-
-    d_proj = dproj_s[...]
-    grad_out[:, : z0 + 2 * inner] = mm(norm_ref[...], d_proj, ((0,), (0,))).astype(BF16)
-    d_normed = mm(d_proj, w_ref[:, : z0 + 2 * inner], ((1,), (1,)))
-    dn_out[...] = d_normed.astype(BF16)
-    hid = hid_ref[...].astype(F32)
+    sl_s[taps + 2 : taps + 3, :lanes] = jnp.sum(d_u, axis=0, keepdims=True)
+    sl_s[taps + 3 : taps + 4, :lanes] = rate * jnp.sum(d_log * step_s[...], axis=0, keepdims=True)
+    sl_s[taps + 4 : taps + 5, :lanes] = d_skip
+    go(sl_s, sl_c, scs.at[0], scr.at[0], c_peer)
+    for k in zorder[:2]:
+        z_send(Z, k)
+    for k in zorder:
+        x_send(X, k)
+    d_normed = mm(dz_b[...], az[...], ((1,), (1,))) + mm(dx_b[...], ax[...], ((1,), (1,)))
+    d_normed = d_normed + mm(dbd_b[...], abd[...], ((1,), (1,)))
+    dn_s[...] = d_normed.astype(BF16)
+    for k in range(1, nt):
+        y_go(4, dn_s.at[token_rows((t + k) % nt)], dn_got.at[t], k)
+    hid = h_all[...].astype(F32)
     rms = lax.rsqrt(jnp.mean(hid * hid, axis=1, keepdims=True) + epsilon)
-    sh_out[taps + 1 : taps + 2, :] = jnp.sum(d_normed * (hid * rms), axis=0, keepdims=True)
-
-
-def prepare_body(heads, bc_width, z0, inner, wz, wx, wbc, wdt, wout, seg, nw, cxb, gnw, cbb, dtb, alog,
-                 dskip, pack, vec, segc):
-    rows = wz.shape[0]
-    pack[:, :bc_width] = wbc[...]
-    pack[:, bc_width:z0] = jnp.zeros((rows, z0 - bc_width), BF16)
-    pack[:, bc_width : bc_width + heads] = wdt[...]
-    pack[:, z0 : z0 + inner] = wz[...]
-    pack[:, z0 + inner : z0 + 2 * inner] = wx[...]
-    pack[:, z0 + 2 * inner :] = wout[...]
-    vec[...] = jnp.zeros(vec.shape, F32)
-    for i, ref in enumerate((nw, cxb, gnw, cbb, dtb, alog, dskip)):
-        vec[i : i + 1, : ref.shape[0]] = ref[...][None, :]
-    segc[...] = jnp.broadcast_to(seg[...].astype(F32), (128, seg.shape[1])).T
-
-
-def prepare(w_z, w_x, w_bc, w_dt, w_out, segments, vectors, z0):
-    rows, inner = w_z.shape
-    width = max(inner, max(v.shape[0] for v in vectors))
-    length = segments.shape[1]
+    ss_s[taps + 1 : taps + 2, :] = jnp.sum(d_normed * (hid * rms), axis=0, keepdims=True)
+    ss_t[pl.ds(t, 1)] = ss_s[...][None]
+    for k in range(1, nt):
+        y_go(5, ss_s, ss_t.at[t], k)
+    arrived(sl_c, scs.at[0], scr.at[0], c_peer)
+    sl_xput[...] = sl_s[...] + sl_c[...]
+    go(sl_xput, sl_x, sxs.at[0], sxr.at[0], x_peer)
+    for k in zorder[2:]:
+        z_send(Z, k)
+    for k in range(1, nt):
+        y_got(5, ss_t.at[(t + nt - k) % nt], k)
+    total = ss_t[0]
+    for i in range(1, nt):
+        total = total + ss_t[i]
+    ss_cput[...] = total
+    go(ss_cput, ss_c, scs.at[1], scr.at[1], c_peer)
+    for k in zorder[:2]:
+        z_send(BD, k)
+    arrived(ss_c, scs.at[1], scr.at[1], c_peer)
+    ss_xput[...] = ss_cput[...] + ss_c[...]
+    go(ss_xput, ss_x, sxs.at[1], sxr.at[1], x_peer)
+    for k in zorder[2:]:
+        z_send(BD, k)
+    z_done(O)
+    for k in range(1, nt):
+        y_got(3, op_got.at[(t + nt - k) % nt], k)
+    total = op_s[token_rows(t), :].astype(F32)
+    for k in range(1, nt):
+        total = total + op_got[(t + nt - k) % nt].astype(F32)
+    op_out[...] = total
+    for k in zorder[:1]:
+        z_send(X, k)
+    z_done(Z)
+    for k in zorder[1:2]:
+        z_send(X, k)
+    z_done(BD)
+    bc_put[...] = gbd_out[:, :bc_width].astype(BF16)
+    for k in range(1, nt):
+        y_go(6, bc_put, bc_got.at[t], k)
+    for k in range(1, nt):
+        y_got(4, dn_got.at[(t + nt - k) % nt], k)
+    total = dn_s[token_rows(t), :].astype(F32)
+    for k in range(1, nt):
+        total = total + dn_got[(t + nt - k) % nt].astype(F32)
+    dn_out[...] = total
+    for k in zorder[2:]:
+        z_send(X, k)
+    arrived(sl_x, sxs.at[0], sxr.at[0], x_peer)
+    sl_z[pl.ds(z, 1)] = (sl_xput[...] + sl_x[...])[None]
+    arrived(ss_x, sxs.at[1], sxr.at[1], x_peer)
+    ss_z[pl.ds(z, 1)] = (ss_xput[...] + ss_x[...])[None]
+    for k in order:
+        go(sl_z.at[z], sl_z.at[z], szs.at[k], szr.at[k], z_peer[k])
+        go(ss_z.at[z], ss_z.at[z], szs.at[zn + k], szr.at[zn + k], z_peer[k])
+    bc_got[pl.ds(t, 1)] = bc_put[...][None]
+    for k in range(1, nt):
+        y_got(6, bc_got.at[(t + nt - k) % nt], k)
+    total = bc_got[0].astype(F32)
+    for i in range(1, nt):
+        total = total + bc_got[i].astype(F32)
+    gbd_out[:, :bc_width] = total
+    z_done(X)
+    for k in order:
+        arrived(sl_z.at[(z + zn - k) % zn], szs.at[k], szr.at[k], z_peer[k])
+        arrived(ss_z.at[(z + zn - k) % zn], szs.at[zn + k], szr.at[zn + k], z_peer[k])
+    sl_total, ss_total = sl_z[0], ss_z[0]
+    for i in range(1, zn):
+        sl_total = sl_total + sl_z[i]
+        ss_total = ss_total + ss_z[i]
+    sl_out[...] = sl_total
+    ss_out[...] = ss_total
+
+    for copy in started:
+        copy.wait_send()
+    for ti in range(4):
+        for level in range(zn):
+            sent = full[ti].at[slot(level, x, c)]
+            crossed = full[ti].at[slot(level, 1 - x, c)]
+            j = 2 * ti * zn + level
+            remote(sent, sent, axs.at[ti * zn + level], axr.at[ti * zn + level], x_peer).wait_send()
+            remote(sent, sent, acs.at[j], acr.at[j], c_peer).wait_send()
+            remote(crossed, crossed, acs.at[j + zn], acr.at[j + zn], c_peer).wait_send()
+
+            @pl.when((level <= z) & has_above)
+            def _(j=j, ti=ti, level=level, sent=sent):
+                remote(sent, sent, azs.at[j], azr.at[ti * zn + level], above).wait_send()
+
+            @pl.when((level >= z) & has_below)
+            def _(j=j, ti=ti, level=level, sent=sent):
+                remote(sent, sent, azs.at[j + zn], azr.at[ti * zn + level], below).wait_send()
+
+
+def mega(w_bd, w_x, w_z, w_o, hidden, cot, seg_col, segments, conv_x_w, conv_bc_w, vec, heads, inner_all,
+         bc_width):
+    n, nt = lax.axis_size("dp"), lax.axis_size("tensor")
+    zn = n // 4
+    rows, inner = w_x.shape
+    own_rows, width = hidden.shape
+    length = nt * own_rows
+    taps = conv_x_w.shape[0]
+    bd = w_bd.shape[1]
+    lanes = bd - bc_width
+    sl, ss = (taps + 5, inner), (taps + 2, width)
+    V = pltpu.VMEM
+    wide = (bd, inner, inner, inner)
+
+    def sds(*shape):
+        return jax.ShapeDtypeStruct(shape, F32)
+
+    def each(*lead):
+        return [V(lead + (cols,), BF16) for cols in wide]
+
+    act = V((length, inner), F32)
+    act_b = V((length, inner), BF16)
     return pl.pallas_call(
-        partial(prepare_body, w_dt.shape[1], w_bc.shape[1], z0, inner),
+        partial(mega_body, n, nt, heads, inner_all, bc_width),
         out_shape=(
-            jax.ShapeDtypeStruct((rows, z0 + 3 * inner), BF16),
-            jax.ShapeDtypeStruct((8, width), F32),
-            jax.ShapeDtypeStruct((length, 128), F32),
+            sds(rows, bd), sds(rows, inner), sds(rows, inner), sds(rows, inner), sds(own_rows, width),
+            sds(own_rows, width), sds(*sl), sds(*ss), sds(length, 128),
         ),
-        in_specs=[VM] * 13,
-        out_specs=(VM,) * 3,
-        name="prepare",
-    )(w_z, w_x, w_bc, w_dt, w_out.T, segments, *vectors)
-
-
-def fused_core(w_full, hid, cot, segments, seg_col, conv_x_w, conv_bc_w, vec, heads, inner,
-               inner_all, bc_width, z0):
-    length, width = hid.shape
-    taps = conv_x_w.shape[0]
-
-    def sds(shape, dtype=F32):
-        return jax.ShapeDtypeStruct(shape, dtype)
-
-    small = (conv_x_w, conv_bc_w, vec)
-    cols = z0 + 2 * inner
-    saved = pl.pallas_call(
-        partial(core_fwd_body, heads, inner, bc_width, z0),
-        out_shape=(sds((length, cols)), sds((length, inner)), sds((length, inner)),
-                   sds((length, width), BF16), sds((8, length))),
-        in_specs=[VM] * 8,
-        out_specs=(VM,) * 5,
-        name="core_fwd",
-    )(w_full, hid, cot, seg_col, segments, *small)
-    sums = tensor_sum(saved[4])
-    return pl.pallas_call(
-        partial(core_bwd_body, heads, inner, inner_all, bc_width, z0),
-        out_shape=(sds(w_full.shape, BF16), sds((length, width), BF16), sds((length, width), BF16),
-                   sds((taps + 5, inner)), sds((taps + 2, width)), sds((length, 128))),
-        in_specs=[VM] * 13,
-        out_specs=(VM,) * 6,
-        scratch_shapes=[pltpu.VMEM((length, inner), F32), pltpu.VMEM((length, inner), F32),
-                        pltpu.VMEM((length, cols), BF16)],
-        name="core_bwd",
-    )(w_full, hid, cot, seg_col, segments, *small, *saved[:4], sums)
-
-
-def finish_body(heads, bc_width, z0, inner, taps, g, dn, op, sl, ss, hidden, cot, gate, vec,
+        in_specs=[VM] * 11,
+        out_specs=(VM,) * 9,
+        scratch_shapes=[
+            *each(n * rows), V((length, width), BF16), V((length, width), BF16),
+            V((length, bd), F32), act, act, act, act, act, act_b, V((length, bc_width), F32),
+            V((length, bc_width), BF16), V((length, lanes), F32), V((length, lanes), F32),
+            V((length, lanes), F32), V((length, length), F32), V((heads, length, length), F32), act, act,
+            act, act, act, act_b, V((nt, 8, length), F32), V((length, width), BF16),
+            act, act, act_b, act_b, V((length, bd), BF16),
+            *each(n * rows), *each(2 * zn, rows), *each(zn, rows), *each(zn, rows), *each(zn, rows),
+            *each(zn, rows),
+            V((length, width), BF16), V((length, width), BF16), V((nt, own_rows, width), BF16),
+            V((nt, own_rows, width), BF16), V((rows, bc_width), BF16), V((nt, rows, bc_width), BF16),
+            V(sl, F32), V(ss, F32), V(sl, F32), V(sl, F32), V(sl, F32), V((zn,) + sl, F32),
+            V((nt,) + ss, F32), V(ss, F32), V(ss, F32), V(ss, F32), V(ss, F32), V((zn,) + ss, F32),
+            DMA((8 * zn,)), DMA((4 * zn,)), DMA((4 * zn,)), DMA((4 * zn,)), DMA((8 * zn,)), DMA((8 * zn,)),
+            DMA((7 * nt,)), DMA((7 * nt,)), DMA((8 * zn,)), DMA((8 * zn,)), DMA((4 * zn,)), DMA((4 * zn,)),
+            DMA((4 * zn,)), DMA((4 * zn,)), DMA((2,)), DMA((2,)), DMA((2,)), DMA((2,)),
+            DMA((2 * zn,)), DMA((2 * zn,)),
+        ],
+        compiler_params=pltpu.CompilerParams(collective_id=3, has_side_effects=True),
+        name="mega",
+    )(w_bd, w_x, w_z, w_o, hidden, cot, seg_col, segments, conv_x_w, conv_bc_w, vec)
+
+
+def finish_body(heads, bc_width, taps, gbd, gxs, gzs, gos, dn, op, sl, ss, hidden, cot, gate, vec,
                 block, ghid, gnorm_in, gz, gx, gbc, gdt, gcxw, gcxb, gcbw, gcbb, gdtb, galog, gskip,
                 ggn, gout):
     rows, width = hidden.shape
@@ -785,11 +1111,13 @@
         + rms * d_scaled
         - cube * hid * jnp.mean(d_scaled * hid, axis=1, keepdims=True)
     )
-    gbc[...] = g[:, :bc_width]
-    gdt[...] = g[:, bc_width : bc_width + heads]
-    gz[...] = g[:, z0 : z0 + inner]
-    gx[...] = g[:, z0 + inner : z0 + 2 * inner]
-    gout[...] = g[:, z0 + 2 * inner :]
+    own, lanes = gbd.shape[0], gbd.shape[1] - bc_width
+    gbc[...] = gbd[:, :bc_width]
+    fill = jnp.zeros((-own % 128, lanes), F32)
+    gdt[...] = jnp.concatenate([gbd[:, bc_width:], fill], axis=0).T[:heads, :own]
+    gz[...] = gzs[...]
+    gx[...] = gxs[...]
+    gout[...] = gos[...]
     gcxw[...] = sl[:taps]
     gcbw[...] = ss[:taps, :bc_width]
     gcxb[...] = sl[taps]
@@ -801,28 +1129,27 @@
     gnorm_in[...] = ss[taps + 1]
 
 
-def finish(g_own, d_normed, out_sum, small_loc, small_sh, hidden, cot, gate, vec, heads, bc_width,
-           z0, inner, taps):
+def finish(summed, hidden, cot, vec, heads, bc_width, taps):
     rows, width = hidden.shape
-    own = g_own.shape[0]
+    own, inner = summed[1].shape
 
     def sds(*shape):
         return jax.ShapeDtypeStruct(shape, F32)
 
     outs = (
         jax.ShapeDtypeStruct((rows, width), BF16), sds(rows, width), sds(width), sds(own, inner),
-        sds(own, inner), sds(own, bc_width), sds(own, heads), sds(taps, inner), sds(inner),
+        sds(own, inner), sds(own, bc_width), sds(heads, own), sds(taps, inner), sds(inner),
         sds(taps, bc_width), sds(bc_width), sds(heads), sds(heads), sds(heads), sds(inner),
         sds(own, inner),
     )
     results = pl.pallas_call(
-        partial(finish_body, heads, bc_width, z0, inner, taps),
+        partial(finish_body, heads, bc_width, taps),
         out_shape=outs,
-        in_specs=[VM] * 9,
+        in_specs=[VM] * 12,
         out_specs=(VM,) * 16,
         name="finish",
-    )(g_own, d_normed, out_sum, small_loc, small_sh, hidden, cot, gate, vec)
-    return (*results[:-1], results[-1].T)
+    )(*summed[:8], hidden, cot, summed[8], vec)
+    return (*results[:6], results[6].T, *results[7:-1], results[-1].T)
 
 
 def per_device(
@@ -844,89 +1171,86 @@
         and w_out.shape[1] <= 128
     )
     if fused:
-        w_pack, vec, seg_col = prepare(
-            w_z, w_x, w_bc, w_dt, w_out, segment_ids,
-            (norm_weight, conv_x_b, gnorm_weight, conv_bc_b, dt_bias, a_log, d_skip), z0,
+        w_bd, vec, seg_col = prepare(
+            w_bc, w_dt, segment_ids,
+            (norm_weight, conv_x_b, gnorm_weight, conv_bc_b, dt_bias, a_log, d_skip), dt_pad,
         )
-    else:
-        w_pack = jnp.concatenate([w_bc, pad_columns(w_dt, dt_pad), w_z, w_x, w_out.T], axis=1)
+        summed = mega(
+            w_bd, w_x, w_z, w_out.T, hidden_in, out_grad, seg_col, segment_ids, conv_x_w, conv_bc_w,
+            vec, heads, inner_all, bc_width,
+        )
+        return finish(summed, hidden_in, out_grad, vec, heads, bc_width, conv_x_w.shape[0])
+    w_pack = jnp.concatenate([w_bc, pad_columns(w_dt, dt_pad), w_z, w_x, w_out.T], axis=1)
     w_all, hid_all, cot_all = gather_all(w_pack, hidden_in, out_grad)
     w_full = w_all.reshape(width, -1)
     w_cat = w_full[:, : z0 + 2 * inner_loc]
     w_out_t = w_full[:, z0 + 2 * inner_loc :]
     cot_all = cot_all.reshape(tokens, width)
     hid_all = hid_all.reshape(tokens, width)
-    if fused:
-        grads, dn_part, out_part, small_loc, small_sh, gate_all = fused_core(
-            w_full, hid_all, cot_all, segment_ids, seg_col, conv_x_w, conv_bc_w, vec, heads,
-            inner_loc, inner_all, bc_width, z0,
+    hid_all = hid_all.astype(F32)
+    rms_all = lax.rsqrt(jnp.mean(hid_all * hid_all, axis=1, keepdims=True) + epsilon)
+    unit_all = hid_all * rms_all
+    normed_all = (unit_all * norm_weight[None, :]).astype(BF16)
+    projected_all = jnp.dot(normed_all, w_cat, preferred_element_type=F32)
+    bc_proj = projected_all[:, :bc_width]
+    dt_proj = projected_all[:, bc_width : bc_width + heads]
+    z_proj = projected_all[:, z0 : z0 + inner_loc]
+    x_proj = projected_all[:, z0 + inner_loc : z0 + 2 * inner_loc]
+    back_proj = jnp.dot(cot_all, w_out_t, preferred_element_type=F32)
+    core_fn = partial(mixer_core, segments=segment_ids[0], block_len=GROUP)
+    gated, core_vjp = jax.vjp(
+        core_fn, z_proj, x_proj, bc_proj, dt_proj, conv_x_w, conv_x_b, conv_bc_w, conv_bc_b,
+        dt_bias, a_log, d_skip,
+    )
+    back_gated = back_proj * gated
+    sums = tensor_sum(
+        jnp.stack(
+            [jnp.sum(gated * gated, axis=1), jnp.sum(back_gated * gnorm_weight[None, :], axis=1)]
         )
-        grads = grads.reshape(n, width // n, -1)
-    else:
-        hid_all = hid_all.astype(F32)
-        rms_all = lax.rsqrt(jnp.mean(hid_all * hid_all, axis=1, keepdims=True) + epsilon)
-        unit_all = hid_all * rms_all
-        normed_all = (unit_all * norm_weight[None, :]).astype(BF16)
-        projected_all = jnp.dot(normed_all, w_cat, preferred_element_type=F32)
-        bc_proj = projected_all[:, :bc_width]
-        dt_proj = projected_all[:, bc_width : bc_width + heads]
-        z_proj = projected_all[:, z0 : z0 + inner_loc]
-        x_proj = projected_all[:, z0 + inner_loc : z0 + 2 * inner_loc]
-        back_proj = jnp.dot(cot_all, w_out_t, preferred_element_type=F32)
-        core_fn = partial(mixer_core, segments=segment_ids[0], block_len=GROUP)
-        gated, core_vjp = jax.vjp(
-            core_fn, z_proj, x_proj, bc_proj, dt_proj, conv_x_w, conv_x_b, conv_bc_w, conv_bc_b,
-            dt_bias, a_log, d_skip,
-        )
-        back_gated = back_proj * gated
-        sums = tensor_sum(
-            jnp.stack(
-                [jnp.sum(gated * gated, axis=1), jnp.sum(back_gated * gnorm_weight[None, :], axis=1)]
-            )
-        )
-        inv_gate = lax.rsqrt(sums[0] / inner_all + epsilon)
-        cube_gate = inv_gate * inv_gate * inv_gate
-        grad_gnorm = jnp.sum(inv_gate[:, None] * back_gated, axis=0)
-        scaled_in = (gated * gnorm_weight[None, :]).astype(BF16)
-        out_part = lax.dot_general(
-            scaled_in, w_out_t, (((1,), (1,)), ((), ())), preferred_element_type=F32
-        ).astype(BF16)
-        d_gated = (inv_gate[:, None] * back_proj) * gnorm_weight[None, :] - (
-            sums[1] * cube_gate / inner_all
-        )[:, None] * gated
-        scaled_out = (inv_gate[:, None] * scaled_in.astype(F32)).astype(BF16)
-        core_grads = core_vjp(d_gated)
-        d_z, d_x, d_bc, d_dt = [part.astype(BF16) for part in core_grads[:4]]
-        d_proj = jnp.concatenate([d_bc, pad_columns(d_dt, dt_pad), d_z, d_x], axis=1)
-        grad_wcat = lax.dot_general(
-            normed_all, d_proj, (((0,), (0,)), ((), ())), preferred_element_type=F32
-        ).astype(BF16)
-        grad_wout_t = lax.dot_general(
-            cot_all, scaled_out, (((0,), (0,)), ((), ())), preferred_element_type=F32
-        ).astype(BF16)
-        dn_part = lax.dot_general(
-            d_proj, w_cat, (((1,), (1,)), ((), ())), preferred_element_type=F32
-        )
-        norm_part = jnp.sum(dn_part * unit_all, axis=0)
-        grads = jnp.concatenate([grad_wcat, grad_wout_t], axis=1).reshape(n, width // n, -1)
-        small_loc = jnp.concatenate(
-            [
-                core_grads[4],
-                core_grads[5][None, :],
-                grad_gnorm[None, :],
-                *[pad_columns(core_grads[i][None, :], inner_loc) for i in (8, 9, 10)],
-            ],
-            axis=0,
-        )
-        small_sh = jnp.concatenate(
-            [
-                pad_columns(core_grads[6], width),
-                pad_columns(core_grads[7][None, :], width),
-                norm_part[None, :],
-            ],
-            axis=0,
-        )
-        dn_part, gate_all = dn_part.astype(BF16), inv_gate[:, None]
+    )
+    inv_gate = lax.rsqrt(sums[0] / inner_all + epsilon)
+    cube_gate = inv_gate * inv_gate * inv_gate
+    grad_gnorm = jnp.sum(inv_gate[:, None] * back_gated, axis=0)
+    scaled_in = (gated * gnorm_weight[None, :]).astype(BF16)
+    out_part = lax.dot_general(
+        scaled_in, w_out_t, (((1,), (1,)), ((), ())), preferred_element_type=F32
+    ).astype(BF16)
+    d_gated = (inv_gate[:, None] * back_proj) * gnorm_weight[None, :] - (
+        sums[1] * cube_gate / inner_all
+    )[:, None] * gated
+    scaled_out = (inv_gate[:, None] * scaled_in.astype(F32)).astype(BF16)
+    core_grads = core_vjp(d_gated)
+    d_z, d_x, d_bc, d_dt = [part.astype(BF16) for part in core_grads[:4]]
+    d_proj = jnp.concatenate([d_bc, pad_columns(d_dt, dt_pad), d_z, d_x], axis=1)
+    grad_wcat = lax.dot_general(
+        normed_all, d_proj, (((0,), (0,)), ((), ())), preferred_element_type=F32
+    ).astype(BF16)
+    grad_wout_t = lax.dot_general(
+        cot_all, scaled_out, (((0,), (0,)), ((), ())), preferred_element_type=F32
+    ).astype(BF16)
+    dn_part = lax.dot_general(
+        d_proj, w_cat, (((1,), (1,)), ((), ())), preferred_element_type=F32
+    )
+    norm_part = jnp.sum(dn_part * unit_all, axis=0)
+    grads = jnp.concatenate([grad_wcat, grad_wout_t], axis=1).reshape(n, width // n, -1)
+    small_loc = jnp.concatenate(
+        [
+            core_grads[4],
+            core_grads[5][None, :],
+            grad_gnorm[None, :],
+            *[pad_columns(core_grads[i][None, :], inner_loc) for i in (8, 9, 10)],
+        ],
+        axis=0,
+    )
+    small_sh = jnp.concatenate(
+        [
+            pad_columns(core_grads[6], width),
+            pad_columns(core_grads[7][None, :], width),
+            norm_part[None, :],
+        ],
+        axis=0,
+    )
+    dn_part, gate_all = dn_part.astype(BF16), inv_gate[:, None]
     g_own, d_normed, out_sum, small_loc, small_sh = reduce_all(
         grads,
         dn_part.reshape(nt, rows_own, width),
@@ -935,12 +1259,6 @@
         small_sh,
         bc_width,
     )
-    taps = conv_x_w.shape[0]
-    if fused:
-        return finish(
-            g_own, d_normed, out_sum, small_loc, small_sh, hidden_in, out_grad, gate_all, vec, heads,
-            bc_width, z0, inner_loc, taps,
-        )
     row_start = lax.axis_index("tensor") * rows_own
     hidden_f = hidden_in.astype(F32)
     inv_rms = lax.rsqrt(jnp.mean(hidden_f * hidden_f, axis=1, keepdims=True) + epsilon)

time: 114 us -> 83.6 us (0.73)
  Pallas kernels: 110 us -> 82.6 us
  local copies, waits for them, and re-layouts: 2.79 us -> 0 us
    pallas_call x7 -> x3, Pallas kernels: 110 us -> 82.6 us  [the longest x1 78.2 us: mega(): pl.pallas_call(partial(mega_body, n, nt, heads, inner_all, bc_width), out...]
    unnamed x2 -> x0, local copies, waits for them, and re-layouts: 2.79 us -> none
where the time goes in v1:
time: 83.6 us; the launch traced here: 83.4 us
  Pallas kernels  82.6 us (99%)
    pallas_call x1, Pallas kernels, mega(): pl.pallas_call(partial(mega_body, n, nt, heads, inner_all, bc_width), out...  78.2 us
    pallas_call x1, Pallas kernels, finish(): pl.pallas_call(partial(finish_body, heads, bc_width, taps), out_shape=out...  2.73 us

profile of v1, /device:TPU:0, one launch (start us, length us, event | category | flops | bytes accessed | tf_op | source)
XLA Modules:
  0.0 83.4 jit_solution(4835431848227365822)
XLA Ops:
  0.6 1.6 %prepare.1 = (bf16[48,384]{1,0:T(8,128)(2,1)}, f32[8,768]{1,0:T(8,128)}, f32[256,128]{1,0:T(8,128)}) custom-call(bf16[48,256]{1,0:T(8,128)(2,1)} %wbc.1, bf16[12,48]{1,0:T(8,128)(2,1)} %bitcast.5, s32[1,256]{1,0:T(1,128)} %refs_7_.1, f32[768]{0:T(1024)} %nw.1, f32[768]{0:T(1024)} %cxb.1, f32[768]{0:T(1024)} %gnw.1, f32[256]{0:T(256)} %cbb.1, f32[12]{0:T(128)} %dtb.1, ...), custom_call_target="tpu_custom_call" | custom-call | tf_op jit(solution)/shard_map/prepare/pallas_call | solution.py:553
  2.3 78.2 %mega.1 = (f32[48,384]{1,0:T(8,128)}, f32[48,768]{1,0:T(8,128)}, f32[48,768]{1,0:T(8,128)}, f32[48,768]{1,0:T(8,128)}, f32[128,768]{1,0:T(8,128)}, /*index=5*/f3...) custom-call(bf16[48,384]{1,0:T(8,128)(2,1)} %get-tuple-element.44.refs_0_, ...), custom_call_target="tpu_custom_call" | custom-call | tf_op jit(solution)/shard_map/mega/pallas_call | solution.py:1068
  80.5 2.7 %finish.1 = (bf16[128,768]{1,0:T(8,128)(2,1)}, f32[128,768]{1,0:T(8,128)}, f32[768]{0:T(1024)}, f32[48,768]{1,0:T(8,128)}, f32[48,768]{1,0:T(8,128)}, /*index=5*...) custom-call(f32[48,384]{1,0:T(8,128)} %get-tuple-element.47.gbd, ...), custom_call_target="tpu_custom_call" | custom-call | tf_op jit(solution)/shard_map/finish/pallas_call | solution.py:1145
